TPU v7x, 32 devices: a whole 2x2x4 slice. The times are simulated.
32 devices in a mesh: row: 8 (over z, core), col: 4 (over y, x).
Axes of the slice: x: 2, y: 2, z: 4, core: 2. Of those that a mesh axis runs over, the one named last changes fastest.
Arguments:
- observed: int32 [2048, 32, 1024], P('row', None, 'col'), may hold values 0 or 1
- first_factor: float32 [2048, 256], P(('row', 'col')), may hold values from -1.35 to 1.35
- second_factor: float32 [1024, 256], P(('col', 'row')), may hold values from -1.35 to 1.35
- third_factor: float32 [32, 256], replicated, may hold values from -1.35 to 1.35
Outputs:
- first_out: float32 [2048, 256], P(('row', 'col'))
- second_out: float32 [1024, 256], P(('col', 'row'))
- third_out: float32 [32, 256], replicated
All inputs are finite; a program needn't handle non-finite values. No bound on the sum of `observed` on one device may be relied on, other than what follows from the above.
Results may differ from a plain program's by a relative error of at most 0.0003.
Values sent between devices are 32-bit elements; how exact they have to be, the bound alone decides.
No kernel may reach another device: no remote copies, remote signals or barrier semaphores. Data moves between devices by JAX's collectives and lax.ppermute only.
A program may use at most 128 MiB of HBM per device.

v0:
```python
import functools

import jax
import jax.numpy as jnp
from jax import lax
from jax.experimental import pallas as pl
from jax.experimental.pallas import tpu as pltpu
from jax.sharding import PartitionSpec as P


STEPS = 2
step_rate = 48.0
f32 = jnp.float32
bf16 = jnp.bfloat16
VMEM_BYTES = 24 * 1024 * 1024


def split(x):
    high = x.astype(bf16)
    low = (x - high.astype(f32)).astype(bf16)
    return high, low


def grad_kernel(obs_hbm, a_ref, b_ref, c_ref, ga_ref, gb_ref, gc_ref,
                obs, bt_cat, b_cat, at_cat, gbt, sems, *, depth_block, group):
    depth = c_ref.shape[0]
    blocks = depth // depth_block
    n, _ = a_ref.shape

    lanes = obs.shape[-1]
    panels = obs.shape[1]

    def fetch(g, h):
        first = pl.multiple_of(g * depth_block, depth_block)
        return pltpu.make_async_copy(
            obs_hbm.at[:, pl.ds(first, depth_block), pl.ds(h * lanes, lanes)],
            obs.at[g, h], sems.at[g, h])

    for g in range(blocks):
        for h in range(panels):
            fetch(g, h).start()
    b = b_ref[...]
    bh, bl = split(b)
    b_cat[...] = jnp.concatenate([bh, bl, bh], 0)
    bth, btl = split(b.T)
    bt_cat[...] = jnp.concatenate([bth, btl, bth], 0)
    ath, atl = split(a_ref[...].T)
    at_cat[...] = jnp.concatenate([ath, ath, atl], 1)
    ga_ref[...] = jnp.zeros_like(ga_ref)
    gbt[...] = jnp.zeros_like(gbt)

    def block(g, carry):
        for h in range(panels):
            fetch(g, h).wait()
        flat = [obs.at[g, h].reshape(n * depth_block, lanes) for h in range(panels)]
        a = a_ref[...]
        first = pl.multiple_of(g * depth_block, depth_block)
        ck = c_ref[pl.ds(first, depth_block), :]
        ckt = ck.T
        rows_c = []
        for k0 in range(0, depth_block, group):
            wide = []
            for k in range(k0, k0 + group):
                ph, pw = split(a * ck[k:k + 1, :])
                wide.append(jnp.concatenate([ph, ph, pw], 1))
            logits = jnp.dot(jnp.concatenate(wide, 0), bt_cat[...], preferred_element_type=f32)
            x = jnp.concatenate([
                jnp.concatenate([p[pl.ds(k, n, stride=depth_block), :] for p in flat], 1)
                for k in range(k0, k0 + group)], 0)
            derivative = 0.5 * jnp.tanh(0.5 * logits) + (0.5 - x.astype(f32))
            dh, dw = split(derivative)
            carried = jnp.dot(
                jnp.concatenate([dh, dh, dw], 1), b_cat[...], preferred_element_type=f32)
            total = None
            for q in range(group):
                k = k0 + q
                cq = carried[q * n:(q + 1) * n]
                term = cq * ck[k:k + 1, :]
                total = term if total is None else total + term
                rows_c.append(jnp.sum(cq * a, axis=0, keepdims=True))
            ga_ref[...] += total
            total = None
            for q in range(group):
                k = k0 + q
                dhq = dh[q * n:(q + 1) * n]
                dwq = dw[q * n:(q + 1) * n]
                gt = jnp.dot(
                    at_cat[...], jnp.concatenate([dhq, dwq, dhq], 0), preferred_element_type=f32)
                term = gt * ckt[:, k:k + 1]
                total = term if total is None else total + term
            gbt[...] += total
        gc_ref[pl.ds(first, depth_block), :] = jnp.concatenate(rows_c, 0)
        return carry

    lax.fori_loop(0, blocks, block, 0)
    gb_ref[...] = gbt[...].T


def gradients(observed, a, b, c):
    rows, depth, cols = observed.shape
    rank = a.shape[1]
    depth_block, group, lanes = 8, 2, 128
    here = pl.BlockSpec(memory_space=pltpu.VMEM)
    return pl.pallas_call(
        functools.partial(grad_kernel, depth_block=depth_block, group=group),
        in_specs=[pl.BlockSpec(memory_space=pltpu.HBM), here, here, here],
        out_specs=[here, here, here],
        out_shape=[
            jax.ShapeDtypeStruct((rows, rank), f32),
            jax.ShapeDtypeStruct((cols, rank), f32),
            jax.ShapeDtypeStruct((depth, rank), f32),
        ],
        scratch_shapes=[
            pltpu.VMEM((depth // depth_block, cols // lanes, rows, depth_block, lanes), jnp.int32),
            pltpu.VMEM((3 * rank, cols), bf16), pltpu.VMEM((3 * cols, rank), bf16),
            pltpu.VMEM((rank, 3 * rows), bf16), pltpu.VMEM((rank, cols), f32),
            pltpu.SemaphoreType.DMA((depth // depth_block, cols // lanes)),
        ],
        compiler_params=pltpu.CompilerParams(vmem_limit_bytes=VMEM_BYTES),
        cost_estimate=pl.CostEstimate(
            flops=18 * rows * depth * cols * rank, bytes_accessed=4 * rows * depth * cols,
            transcendentals=rows * depth * cols),
    )(pltpu.with_memory_space_constraint(observed, pltpu.HBM), a, b, c)


def exchange(x, axis, mask):
    n = lax.axis_size(axis)
    return lax.ppermute(x, axis, [(i, i ^ mask) for i in range(n)])


def stage_kernel(a_hbm, b_hbm, c_hbm, a_ref, b_ref, c_ref, sems):
    copies = [
        pltpu.make_async_copy(src, dst, sems.at[i])
        for i, (src, dst) in enumerate(((a_hbm, a_ref), (b_hbm, b_ref), (c_hbm, c_ref)))
    ]
    for copy in copies:
        copy.start()
    for copy in copies:
        copy.wait()


def staged(a, b, c):
    return pl.pallas_call(
        stage_kernel,
        in_specs=[pl.BlockSpec(memory_space=pltpu.HBM)] * 3,
        out_specs=[pl.BlockSpec(memory_space=pltpu.VMEM)] * 3,
        out_shape=[jax.ShapeDtypeStruct(x.shape, x.dtype) for x in (a, b, c)],
        scratch_shapes=[pltpu.SemaphoreType.DMA((3,))],
        compiler_params=pltpu.CompilerParams(vmem_limit_bytes=VMEM_BYTES),
    )(*[pltpu.with_memory_space_constraint(x, pltpu.HBM) for x in (a, b, c)])


def tree_sum(terms):
    while len(terms) > 1:
        terms = [terms[i] + terms[i + 1] for i in range(0, len(terms), 2)]
    return terms[0]


def take(x, index):
    return lax.dynamic_index_in_dim(x, index, 0, keepdims=False)


def in_order(parts, index):
    x = jnp.stack(parts)
    n = x.shape[0]
    width = 1
    while width < n:
        y = x.reshape((n // (2 * width), 2, width) + x.shape[1:])
        flipped = jnp.stack([y[:, 1], y[:, 0]], 1)
        x = jnp.where((index & width) != 0, flipped, y).reshape(x.shape)
        width *= 2
    return x


def per_device(observed, first_factor, second_factor, third_factor):
    row_count = lax.axis_size("row")
    col_count = lax.axis_size("col")
    chip_count = row_count // 2
    for n in (chip_count, col_count):
        assert n & (n - 1) == 0
    rows_here, depth_count, cols_here = observed.shape
    rank = third_factor.shape[1]
    rows_own, cols_own = first_factor.shape[0], second_factor.shape[0]
    half_depth = depth_count // 2
    cols_half = cols_here // 2
    row = lax.axis_index("row")
    col = lax.axis_index("col")
    core, chip = row & 1, row >> 1
    rate_one = step_rate / (cols_here * col_count * depth_count)
    rate_two = step_rate / (rows_here * row_count * depth_count)
    rate_three = step_rate / (rows_here * row_count * cols_here * col_count)
    chip_masks = []
    bit = 1
    while bit < chip_count:
        chip_masks.append(bit | (bit >> 1))
        bit *= 2

    def gather_rows(own, sent):
        parts = [own] + [exchange(sent, "col", s) for s in range(1, col_count)]
        return in_order(parts, col).reshape(rows_here, rank)

    def both_cores(half, depth_half):
        other = exchange(jnp.concatenate([half.reshape(cols_half, rank), depth_half]), "row", 1)
        other_half = other[:cols_half].reshape(half.shape)
        other_depth = other[cols_half:]
        wide = jnp.where(core == 0, jnp.stack([half, other_half], 1), jnp.stack([other_half, half], 1))
        depth = jnp.where(core == 0, jnp.concatenate([depth_half, other_depth]),
                          jnp.concatenate([other_depth, depth_half]))
        return wide.reshape(cols_here, rank), depth

    a, b, c = staged(first_factor, second_factor, third_factor)
    c_half = lax.dynamic_slice_in_dim(c, core * half_depth, half_depth, 0)
    held = [b]
    places = [0]
    mask = chip_count // 2
    while mask:
        sent = jnp.stack(held) if len(held) > 1 else second_factor[None]
        got = exchange(sent, "row", 2 * mask)
        held = held + [got[i] for i in range(len(held))]
        places = places + [p ^ mask for p in places]
        mask //= 2
    b_half = in_order([held[places.index(s)] for s in range(chip_count)], chip)
    wide_a = gather_rows(a, first_factor)
    wide_b, c = both_cores(b_half, c_half)
    for iteration in range(STEPS):
        last = iteration == STEPS - 1
        ga, gb, gc = gradients(observed, wide_a, wide_b, c)
        ga = ga.reshape(col_count, rows_own, rank)
        gb = gb.reshape(chip_count, 2, cols_own, rank)
        gc = gc.reshape(2, half_depth, rank)
        pick = lambda x, axis, which: lax.dynamic_index_in_dim(x, which, axis, keepdims=False)
        got = exchange(
            jnp.concatenate([pick(gb, 1, 1 - core).reshape(cols_half, rank), pick(gc, 0, 1 - core)]), "row", 1)
        gb = pick(gb, 1, core) + got[:cols_half].reshape(chip_count, cols_own, rank)
        gc = pick(gc, 0, core) + got[cols_half:]
        parts = [jnp.concatenate([take(ga, col), gc])]
        for s in range(1, col_count):
            parts.append(exchange(jnp.concatenate([take(ga, col ^ s), gc]), "col", s))
        both = tree_sum(parts)
        a = a - rate_one * both[:rows_own]
        gc = both[rows_own:]
        if last:
            parts = [jnp.concatenate([take(gb, chip), gc])]
            for s in range(1, chip_count):
                parts.append(exchange(jnp.concatenate([take(gb, chip ^ s), gc]), "row", 2 * s))
            both = tree_sum(parts)
            b = take(b_half, chip) - rate_two * both[:cols_own]
            c_half = c_half - rate_three * both[cols_own:]
            other = exchange(c_half, "row", 1)
            c = jnp.where(core == 0, jnp.concatenate([c_half, other]), jnp.concatenate([other, c_half]))
        else:
            both = jnp.concatenate([gb.reshape(cols_half, rank), gc])
            for mask in chip_masks:
                both = both + exchange(both, "row", 2 * mask)
            wide_a = gather_rows(a, a)
            b_half = b_half - rate_two * both[:cols_half].reshape(b_half.shape)
            c_half = c_half - rate_three * both[cols_half:]
            wide_b, c = both_cores(b_half, c_half)
    return (a, b, c)


def solution(mesh):
    return jax.shard_map(
        per_device,
        mesh=mesh,
        in_specs=(P("row", None, "col"), P(("row", "col"), None), P(("col", "row"), None), P()),
        out_specs=(P(("row", "col"), None), P(("col", "row"), None), P()),
        check_vma=False,
    )
```

profile of v0, /device:TPU:0, one launch (start us, length us, event | category | flops | bytes accessed | tf_op | source)
XLA Modules:
  0.0 95.3 jit_solution(3689435990147083023)
XLA Ops:
  0.6 3.0 %collective-permute-start = (f32[64,256]{1,0:T(8,128)}, f32[64,256]{1,0:T(8,128)S(1)}, u32[]{:S(2)}, u32[]{:S(2)}) collective-permute-start(f32[64,256]{1,0:T(8,128)} %a_hbm.1), channel_id=1, source_target_pairs={{0,1},{1,0},{2,3},{3,2},{4,5},{5,4},{6,7},{7,6},{8,9},{9,8},{10,11... | collective-permute-start | bytes 196616 | tf_op jit(solution)/shard_map/ppermute | solution.py:128
  3.7 1.5 %collective-permute-start.1 = (f32[64,256]{1,0:T(8,128)}, f32[64,256]{1,0:T(8,128)S(1)}, u32[]{:S(2)}, u32[]{:S(2)}) collective-permute-start(f32[64,256]{1,0:T(8,128)} %a_hbm.1), channel_id=1, source_target_pairs={{0,2},{1,3},{2,0},{3,1},{4,6},{5,7},{6,4},{7,5},{8,10},{9,11},{10,... | collective-permute-start | bytes 196616 | tf_op jit(solution)/shard_map/ppermute | solution.py:128
  5.2 3.0 %collective-permute-start.3 = (f32[1,32,256]{2,1,0:T(8,128)}, f32[1,32,256]{2,1,0:T(8,128)S(1)}, u32[]{:S(2)}, u32[]{:S(2)}) collective-permute-start(f32[1,32,256]{2,1,0:T(8,128)} %bitcast.181), channel_id=1, source_target_pairs={{0,16},{4,20},{8,24},{12,28},{16,0},{20,4},{24,8},{28,12},{1,17},{... | collective-permute-start | bytes 98312 | tf_op jit(solution)/shard_map/ppermute | solution.py:128
  10.4 1.9 %collective-permute-start.4 = (f32[2,32,256]{2,1,0:T(8,128)S(1)}, f32[2,32,256]{2,1,0:T(8,128)S(1)}, u32[]{:S(2)}, u32[]{:S(2)}) collective-permute-start(f32[2,32,256]{2,1,0:T(8,128)S(1)} %pad_maximum_fusion.26), channel_id=1, source_target_pairs={{0,8},{4,12},{8,0},{12,4},{16,24},{20,28},{24,16},{28,20},{1,9},{5... | collective-permute-start | bytes 196616 | tf_op jit(solution)/shard_map/ppermute | solution.py:128
  12.5 2.1 %collective-permute-done.4 = f32[2,32,256]{2,1,0:T(8,128)S(1)} collective-permute-done((f32[2,32,256]{2,1,0:T(8,128)S(1)}, f32[2,32,256]{2,1,0:T(8,128)S(1)}, u32[]{:S(2)}, u32[]{:S(2)}) %collective-permute-start.4) | collective-permute-done | bytes 65568 | tf_op jit(solution)/shard_map/ppermute | solution.py:128
  14.9 1.3 %collective-permute-done.5 = f32[144,256]{1,0:T(8,128)S(1)} collective-permute-done((f32[144,256]{1,0:T(8,128)S(1)}, f32[144,256]{1,0:T(8,128)S(1)}, u32[]{:S(2)}, u32[]{:S(2)}) %collective-permute-start.5) | collective-permute-done | bytes 147488 | tf_op jit(solution)/shard_map/ppermute | solution.py:128
  16.3 15.3 %shard_map.68 = (f32[256,256]{1,0:T(8,128)S(1)}, f32[256,256]{1,0:T(8,128)S(1)}, f32[32,256]{1,0:T(8,128)S(1)}) custom-call(s32[256,32,256]{2,1,0:T(8,128)} %obs_hbm.3, f32[256,256]{1,0:T(8,128)S(1)} %fusion.1.a_ref, f32[256,256]{1,0:T(8,128)S(1)} %bitcast.145, f32[32,256]{1,0:T(8,128)S(1)} %maximum_select_fusion.3.c_ref), custom_call_target="tpu_custom_call" | custom-call | flops 9663676416 | bytes 8388608 | tf_op jit(solution)/shard_map/pallas_call | solution.py:104
  33.1 1.9 %collective-permute-start.7 = (f32[80,256]{1,0:T(8,128)S(1)}, f32[80,256]{1,0:T(8,128)S(1)}, u32[]{:S(2)}, u32[]{:S(2)}) collective-permute-start(f32[80,256]{1,0:T(8,128)S(1)} %get-tuple-element.66), channel_id=1, source_target_pairs={{0,1},{1,0},{2,3},{3,2},{4,5},{5,4},{6,7},{7,6},{8,9},{9,8},{10,11... | collective-permute-start | bytes 245768 | tf_op jit(solution)/shard_map/ppermute | solution.py:128
  35.0 1.5 %collective-permute-start.8 = (f32[80,256]{1,0:T(8,128)S(1)}, f32[80,256]{1,0:T(8,128)S(1)}, u32[]{:S(2)}, u32[]{:S(2)}) collective-permute-start(f32[80,256]{1,0:T(8,128)S(1)} %get-tuple-element.67), channel_id=1, source_target_pairs={{0,2},{1,3},{2,0},{3,1},{4,6},{5,7},{6,4},{7,5},{8,10},{9,11},{10,... | collective-permute-start | bytes 245768 | tf_op jit(solution)/shard_map/ppermute | solution.py:128
  37.7 2.5 %collective-permute-done.8 = f32[80,256]{1,0:T(8,128)S(1)} collective-permute-done((f32[80,256]{1,0:T(8,128)S(1)}, f32[80,256]{1,0:T(8,128)S(1)}, u32[]{:S(2)}, u32[]{:S(2)}) %collective-permute-start.8) | collective-permute-done | bytes 81952 | tf_op jit(solution)/shard_map/ppermute | solution.py:128
  40.3 1.6 %collective-permute-done.9 = f32[80,256]{1,0:T(8,128)S(1)} collective-permute-done((f32[80,256]{1,0:T(8,128)S(1)}, f32[80,256]{1,0:T(8,128)S(1)}, u32[]{:S(2)}, u32[]{:S(2)}) %collective-permute-start.9) | collective-permute-done | bytes 81952 | tf_op jit(solution)/shard_map/ppermute | solution.py:128
  43.3 2.2 %collective-permute-start.12 = (f32[64,256]{1,0:T(8,128)S(1)}, f32[64,256]{1,0:T(8,128)S(1)}, u32[]{:S(2)}, u32[]{:S(2)}) collective-permute-start(f32[64,256]{1,0:T(8,128)S(1)} %fusion.9), channel_id=1, source_target_pairs={{0,3},{1,2},{2,1},{3,0},{4,7},{5,6},{6,5},{7,4},{8,11},{9,10},{10,... | collective-permute-start | bytes 196616 | tf_op jit(solution)/shard_map/ppermute | solution.py:128
  45.5 1.6 %collective-permute-start.13 = (f32[144,256]{1,0:T(8,128)S(1)}, f32[144,256]{1,0:T(8,128)S(1)}, u32[]{:S(2)}, u32[]{:S(2)}) collective-permute-start(f32[144,256]{1,0:T(8,128)S(1)} %pad_maximum_fusion.16), channel_id=1, source_target_pairs={{0,8},{4,12},{8,0},{12,4},{16,24},{20,28},{24,16},{28,20},{1,9},{5... | collective-permute-start | bytes 442376 | tf_op jit(solution)/shard_map/ppermute | solution.py:128
  47.1 1.3 %collective-permute-done.12 = f32[64,256]{1,0:T(8,128)S(1)} collective-permute-done((f32[64,256]{1,0:T(8,128)S(1)}, f32[64,256]{1,0:T(8,128)S(1)}, u32[]{:S(2)}, u32[]{:S(2)}) %collective-permute-start.12) | collective-permute-done | bytes 65568 | tf_op jit(solution)/shard_map/ppermute | solution.py:128
  48.5 2.1 %collective-permute-done.13 = f32[144,256]{1,0:T(8,128)S(1)} collective-permute-done((f32[144,256]{1,0:T(8,128)S(1)}, f32[144,256]{1,0:T(8,128)S(1)}, u32[]{:S(2)}, u32[]{:S(2)}) %collective-permute-start.13) | collective-permute-done | bytes 147488 | tf_op jit(solution)/shard_map/ppermute | solution.py:128
  50.7 3.9 %collective-permute-start.14 = (f32[144,256]{1,0:T(8,128)S(1)}, f32[144,256]{1,0:T(8,128)S(1)}, u32[]{:S(2)}, u32[]{:S(2)}) collective-permute-start(f32[144,256]{1,0:T(8,128)S(1)} %fusion.17), channel_id=1, source_target_pairs={{0,24},{4,28},{8,16},{12,20},{16,8},{20,12},{24,0},{28,4},{1,25},{... | collective-permute-start | bytes 442376 | tf_op jit(solution)/shard_map/ppermute | solution.py:128
  54.7 3.2 %collective-permute-done.14 = f32[144,256]{1,0:T(8,128)S(1)} collective-permute-done((f32[144,256]{1,0:T(8,128)S(1)}, f32[144,256]{1,0:T(8,128)S(1)}, u32[]{:S(2)}, u32[]{:S(2)}) %collective-permute-start.14) | collective-permute-done | bytes 147488 | tf_op jit(solution)/shard_map/ppermute | solution.py:128
  59.4 15.3 %shard_map.69 = (f32[256,256]{1,0:T(8,128)S(1)}, f32[256,256]{1,0:T(8,128)S(1)}, f32[32,256]{1,0:T(8,128)S(1)}) custom-call(s32[256,32,256]{2,1,0:T(8,128)} %obs_hbm.3, f32[256,256]{1,0:T(8,128)S(1)} %fusion.a_ref, f32[256,256]{1,0:T(8,128)S(1)} %bitcast.144, f32[32,256]{1,0:T(8,128)S(1)} %maximum_select_fusion.4.c_ref), custom_call_target="tpu_custom_call" | custom-call | flops 9663676416 | bytes 8388608 | tf_op jit(solution)/shard_map/pallas_call | solution.py:104
  77.7 2.1 %collective-permute-start.19 = (f32[80,256]{1,0:T(8,128)S(1)}, f32[80,256]{1,0:T(8,128)S(1)}, u32[]{:S(2)}, u32[]{:S(2)}) collective-permute-start(f32[80,256]{1,0:T(8,128)S(1)} %get-tuple-element.62), channel_id=1, source_target_pairs={{0,3},{1,2},{2,1},{3,0},{4,7},{5,6},{6,5},{7,4},{8,11},{9,10},{10,... | collective-permute-start | bytes 245768 | tf_op jit(solution)/shard_map/ppermute | solution.py:128
  79.9 1.3 %collective-permute-done.17 = f32[80,256]{1,0:T(8,128)S(1)} collective-permute-done((f32[80,256]{1,0:T(8,128)S(1)}, f32[80,256]{1,0:T(8,128)S(1)}, u32[]{:S(2)}, u32[]{:S(2)}) %collective-permute-start.17) | collective-permute-done | bytes 81952 | tf_op jit(solution)/shard_map/ppermute | solution.py:128
  83.1 1.7 %collective-permute-start.20 = (f32[48,256]{1,0:T(8,128)S(1)}, f32[48,256]{1,0:T(8,128)S(1)}, u32[]{:S(2)}, u32[]{:S(2)}) collective-permute-start(f32[48,256]{1,0:T(8,128)S(1)} %get-tuple-element.60), channel_id=1, source_target_pairs={{0,8},{4,12},{8,0},{12,4},{16,24},{20,28},{24,16},{28,20},{1,9},{5... | collective-permute-start | bytes 147464 | tf_op jit(solution)/shard_map/ppermute | solution.py:128
  84.9 2.6 %collective-permute-start.21 = (f32[48,256]{1,0:T(8,128)S(1)}, f32[48,256]{1,0:T(8,128)S(1)}, u32[]{:S(2)}, u32[]{:S(2)}) collective-permute-start(f32[48,256]{1,0:T(8,128)S(1)} %get-tuple-element.61), channel_id=1, source_target_pairs={{0,16},{4,20},{8,24},{12,28},{16,0},{20,4},{24,8},{28,12},{1,17},{... | collective-permute-start | bytes 147464 | tf_op jit(solution)/shard_map/ppermute | solution.py:128
  88.5 3.0 %collective-permute-done.21 = f32[48,256]{1,0:T(8,128)S(1)} collective-permute-done((f32[48,256]{1,0:T(8,128)S(1)}, f32[48,256]{1,0:T(8,128)S(1)}, u32[]{:S(2)}, u32[]{:S(2)}) %collective-permute-start.21) | collective-permute-done | bytes 49184 | tf_op jit(solution)/shard_map/ppermute | solution.py:128
  91.5 1.9 %collective-permute-done.22 = f32[48,256]{1,0:T(8,128)S(1)} collective-permute-done((f32[48,256]{1,0:T(8,128)S(1)}, f32[48,256]{1,0:T(8,128)S(1)}, u32[]{:S(2)}, u32[]{:S(2)}) %collective-permute-start.22) | collective-permute-done | bytes 49184 | tf_op jit(solution)/shard_map/ppermute | solution.py:128
  (92 shorter events, 16.1 us)
Async XLA Ops:
  0.6 11.6 %collective-permute-start = (f32[64,256]{1,0:T(8,128)}, f32[64,256]{1,0:T(8,128)S(1)}, u32[]{:S(2)}, u32[]{:S(2)}) collective-permute-start(f32[64,256]{1,0:T(8,128)} %a_hbm.1), channel_id=1, source_target_pairs={{0,1},{1,0},{2,3},{3,2},{4,5},{5,4},{6,7},{7,6},{8,9},{9,8},{10,11... | collective-permute-start | bytes 196616 | tf_op jit(solution)/shard_map/ppermute | solution.py:128
  3.7 8.6 %collective-permute-start.1 = (f32[64,256]{1,0:T(8,128)}, f32[64,256]{1,0:T(8,128)S(1)}, u32[]{:S(2)}, u32[]{:S(2)}) collective-permute-start(f32[64,256]{1,0:T(8,128)} %a_hbm.1), channel_id=1, source_target_pairs={{0,2},{1,3},{2,0},{3,1},{4,6},{5,7},{6,4},{7,5},{8,10},{9,11},{10,... | collective-permute-start | bytes 196616 | tf_op jit(solution)/shard_map/ppermute | solution.py:128
  5.2 7.1 %collective-permute-start.2 = (f32[64,256]{1,0:T(8,128)}, f32[64,256]{1,0:T(8,128)S(1)}, u32[]{:S(2)}, u32[]{:S(2)}) collective-permute-start(f32[64,256]{1,0:T(8,128)} %a_hbm.1), channel_id=1, source_target_pairs={{0,3},{1,2},{2,1},{3,0},{4,7},{5,6},{6,5},{7,4},{8,11},{9,10},{10,... | collective-permute-start | bytes 196616 | tf_op jit(solution)/shard_map/ppermute | solution.py:128
  5.2 5.1 %collective-permute-start.3 = (f32[1,32,256]{2,1,0:T(8,128)}, f32[1,32,256]{2,1,0:T(8,128)S(1)}, u32[]{:S(2)}, u32[]{:S(2)}) collective-permute-start(f32[1,32,256]{2,1,0:T(8,128)} %bitcast.181), channel_id=1, source_target_pairs={{0,16},{4,20},{8,24},{12,28},{16,0},{20,4},{24,8},{28,12},{1,17},{... | collective-permute-start | bytes 98312 | tf_op jit(solution)/shard_map/ppermute | solution.py:128
  10.4 4.3 %collective-permute-start.4 = (f32[2,32,256]{2,1,0:T(8,128)S(1)}, f32[2,32,256]{2,1,0:T(8,128)S(1)}, u32[]{:S(2)}, u32[]{:S(2)}) collective-permute-start(f32[2,32,256]{2,1,0:T(8,128)S(1)} %pad_maximum_fusion.26), channel_id=1, source_target_pairs={{0,8},{4,12},{8,0},{12,4},{16,24},{20,28},{24,16},{28,20},{1,9},{5... | collective-permute-start | bytes 196616 | tf_op jit(solution)/shard_map/ppermute | solution.py:128
  14.8 1.4 %collective-permute-start.5 = (f32[144,256]{1,0:T(8,128)S(1)}, f32[144,256]{1,0:T(8,128)S(1)}, u32[]{:S(2)}, u32[]{:S(2)}) collective-permute-start(f32[144,256]{1,0:T(8,128)S(1)} %pad_maximum_fusion.14), channel_id=1, source_target_pairs={{0,4},{4,0},{8,12},{12,8},{16,20},{20,16},{24,28},{28,24},{1,5},{5... | collective-permute-start | bytes 442376 | tf_op jit(solution)/shard_map/ppermute | solution.py:128
  31.6 1.4 %collective-permute-start.6 = (f32[144,256]{1,0:T(8,128)S(1)}, f32[144,256]{1,0:T(8,128)S(1)}, u32[]{:S(2)}, u32[]{:S(2)}) collective-permute-start(f32[144,256]{1,0:T(8,128)S(1)} %pad_maximum_fusion.15), channel_id=1, source_target_pairs={{0,4},{4,0},{8,12},{12,8},{16,20},{20,16},{24,28},{28,24},{1,5},{5... | collective-permute-start | bytes 442376 | tf_op jit(solution)/shard_map/ppermute | solution.py:128
  33.1 4.6 %collective-permute-start.7 = (f32[80,256]{1,0:T(8,128)S(1)}, f32[80,256]{1,0:T(8,128)S(1)}, u32[]{:S(2)}, u32[]{:S(2)}) collective-permute-start(f32[80,256]{1,0:T(8,128)S(1)} %get-tuple-element.66), channel_id=1, source_target_pairs={{0,1},{1,0},{2,3},{3,2},{4,5},{5,4},{6,7},{7,6},{8,9},{9,8},{10,11... | collective-permute-start | bytes 245768 | tf_op jit(solution)/shard_map/ppermute | solution.py:128
  35.0 5.3 %collective-permute-start.8 = (f32[80,256]{1,0:T(8,128)S(1)}, f32[80,256]{1,0:T(8,128)S(1)}, u32[]{:S(2)}, u32[]{:S(2)}) collective-permute-start(f32[80,256]{1,0:T(8,128)S(1)} %get-tuple-element.67), channel_id=1, source_target_pairs={{0,2},{1,3},{2,0},{3,1},{4,6},{5,7},{6,4},{7,5},{8,10},{9,11},{10,... | collective-permute-start | bytes 245768 | tf_op jit(solution)/shard_map/ppermute | solution.py:128
  36.5 5.3 %collective-permute-start.9 = (f32[80,256]{1,0:T(8,128)S(1)}, f32[80,256]{1,0:T(8,128)S(1)}, u32[]{:S(2)}, u32[]{:S(2)}) collective-permute-start(f32[80,256]{1,0:T(8,128)S(1)} %get-tuple-element.65), channel_id=1, source_target_pairs={{0,3},{1,2},{2,1},{3,0},{4,7},{5,6},{6,5},{7,4},{8,11},{9,10},{10,... | collective-permute-start | bytes 245768 | tf_op jit(solution)/shard_map/ppermute | solution.py:128
  41.9 5.2 %collective-permute-start.10 = (f32[64,256]{1,0:T(8,128)S(1)}, f32[64,256]{1,0:T(8,128)S(1)}, u32[]{:S(2)}, u32[]{:S(2)}) collective-permute-start(f32[64,256]{1,0:T(8,128)S(1)} %fusion.9), channel_id=1, source_target_pairs={{0,1},{1,0},{2,3},{3,2},{4,5},{5,4},{6,7},{7,6},{8,9},{9,8},{10,11... | collective-permute-start | bytes 196616 | tf_op jit(solution)/shard_map/ppermute | solution.py:128
  42.5 4.6 %collective-permute-start.11 = (f32[64,256]{1,0:T(8,128)S(1)}, f32[64,256]{1,0:T(8,128)S(1)}, u32[]{:S(2)}, u32[]{:S(2)}) collective-permute-start(f32[64,256]{1,0:T(8,128)S(1)} %fusion.9), channel_id=1, source_target_pairs={{0,2},{1,3},{2,0},{3,1},{4,6},{5,7},{6,4},{7,5},{8,10},{9,11},{10,... | collective-permute-start | bytes 196616 | tf_op jit(solution)/shard_map/ppermute | solution.py:128
  43.3 5.2 %collective-permute-start.12 = (f32[64,256]{1,0:T(8,128)S(1)}, f32[64,256]{1,0:T(8,128)S(1)}, u32[]{:S(2)}, u32[]{:S(2)}) collective-permute-start(f32[64,256]{1,0:T(8,128)S(1)} %fusion.9), channel_id=1, source_target_pairs={{0,3},{1,2},{2,1},{3,0},{4,7},{5,6},{6,5},{7,4},{8,11},{9,10},{10,... | collective-permute-start | bytes 196616 | tf_op jit(solution)/shard_map/ppermute | solution.py:128
  45.5 5.2 %collective-permute-start.13 = (f32[144,256]{1,0:T(8,128)S(1)}, f32[144,256]{1,0:T(8,128)S(1)}, u32[]{:S(2)}, u32[]{:S(2)}) collective-permute-start(f32[144,256]{1,0:T(8,128)S(1)} %pad_maximum_fusion.16), channel_id=1, source_target_pairs={{0,8},{4,12},{8,0},{12,4},{16,24},{20,28},{24,16},{28,20},{1,9},{5... | collective-permute-start | bytes 442376 | tf_op jit(solution)/shard_map/ppermute | solution.py:128
  50.7 7.1 %collective-permute-start.14 = (f32[144,256]{1,0:T(8,128)S(1)}, f32[144,256]{1,0:T(8,128)S(1)}, u32[]{:S(2)}, u32[]{:S(2)}) collective-permute-start(f32[144,256]{1,0:T(8,128)S(1)} %fusion.17), channel_id=1, source_target_pairs={{0,24},{4,28},{8,16},{12,20},{16,8},{20,12},{24,0},{28,4},{1,25},{... | collective-permute-start | bytes 442376 | tf_op jit(solution)/shard_map/ppermute | solution.py:128
  57.9 1.4 %collective-permute-start.15 = (f32[144,256]{1,0:T(8,128)S(1)}, f32[144,256]{1,0:T(8,128)S(1)}, u32[]{:S(2)}, u32[]{:S(2)}) collective-permute-start(f32[144,256]{1,0:T(8,128)S(1)} %pad_maximum_fusion.17), channel_id=1, source_target_pairs={{0,4},{4,0},{8,12},{12,8},{16,20},{20,16},{24,28},{28,24},{1,5},{5... | collective-permute-start | bytes 442376 | tf_op jit(solution)/shard_map/ppermute | solution.py:128
  74.8 1.4 %collective-permute-start.16 = (f32[144,256]{1,0:T(8,128)S(1)}, f32[144,256]{1,0:T(8,128)S(1)}, u32[]{:S(2)}, u32[]{:S(2)}) collective-permute-start(f32[144,256]{1,0:T(8,128)S(1)} %pad_maximum_fusion.18), channel_id=1, source_target_pairs={{0,4},{4,0},{8,12},{12,8},{16,20},{20,16},{24,28},{28,24},{1,5},{5... | collective-permute-start | bytes 442376 | tf_op jit(solution)/shard_map/ppermute | solution.py:128
  76.3 4.9 %collective-permute-start.17 = (f32[80,256]{1,0:T(8,128)S(1)}, f32[80,256]{1,0:T(8,128)S(1)}, u32[]{:S(2)}, u32[]{:S(2)}) collective-permute-start(f32[80,256]{1,0:T(8,128)S(1)} %get-tuple-element.63), channel_id=1, source_target_pairs={{0,1},{1,0},{2,3},{3,2},{4,5},{5,4},{6,7},{7,6},{8,9},{9,8},{10,11... | collective-permute-start | bytes 245768 | tf_op jit(solution)/shard_map/ppermute | solution.py:128
  76.9 5.3 %collective-permute-start.18 = (f32[80,256]{1,0:T(8,128)S(1)}, f32[80,256]{1,0:T(8,128)S(1)}, u32[]{:S(2)}, u32[]{:S(2)}) collective-permute-start(f32[80,256]{1,0:T(8,128)S(1)} %get-tuple-element.64), channel_id=1, source_target_pairs={{0,2},{1,3},{2,0},{3,1},{4,6},{5,7},{6,4},{7,5},{8,10},{9,11},{10,... | collective-permute-start | bytes 245768 | tf_op jit(solution)/shard_map/ppermute | solution.py:128
  77.7 5.3 %collective-permute-start.19 = (f32[80,256]{1,0:T(8,128)S(1)}, f32[80,256]{1,0:T(8,128)S(1)}, u32[]{:S(2)}, u32[]{:S(2)}) collective-permute-start(f32[80,256]{1,0:T(8,128)S(1)} %get-tuple-element.62), channel_id=1, source_target_pairs={{0,3},{1,2},{2,1},{3,0},{4,7},{5,6},{6,5},{7,4},{8,11},{9,10},{10,... | collective-permute-start | bytes 245768 | tf_op jit(solution)/shard_map/ppermute | solution.py:128
  83.1 5.3 %collective-permute-start.20 = (f32[48,256]{1,0:T(8,128)S(1)}, f32[48,256]{1,0:T(8,128)S(1)}, u32[]{:S(2)}, u32[]{:S(2)}) collective-permute-start(f32[48,256]{1,0:T(8,128)S(1)} %get-tuple-element.60), channel_id=1, source_target_pairs={{0,8},{4,12},{8,0},{12,4},{16,24},{20,28},{24,16},{28,20},{1,9},{5... | collective-permute-start | bytes 147464 | tf_op jit(solution)/shard_map/ppermute | solution.py:128
  84.9 6.6 %collective-permute-start.21 = (f32[48,256]{1,0:T(8,128)S(1)}, f32[48,256]{1,0:T(8,128)S(1)}, u32[]{:S(2)}, u32[]{:S(2)}) collective-permute-start(f32[48,256]{1,0:T(8,128)S(1)} %get-tuple-element.61), channel_id=1, source_target_pairs={{0,16},{4,20},{8,24},{12,28},{16,0},{20,4},{24,8},{28,12},{1,17},{... | collective-permute-start | bytes 147464 | tf_op jit(solution)/shard_map/ppermute | solution.py:128
  87.5 5.9 %collective-permute-start.22 = (f32[48,256]{1,0:T(8,128)S(1)}, f32[48,256]{1,0:T(8,128)S(1)}, u32[]{:S(2)}, u32[]{:S(2)}) collective-permute-start(f32[48,256]{1,0:T(8,128)S(1)} %get-tuple-element.59), channel_id=1, source_target_pairs={{0,24},{4,28},{8,16},{12,20},{16,8},{20,12},{24,0},{28,4},{1,25},{... | collective-permute-start | bytes 147464 | tf_op jit(solution)/shard_map/ppermute | solution.py:128
  93.4 1.2 %collective-permute-start.23 = (f32[16,256]{1,0:T(8,128)S(1)}, f32[16,256]{1,0:T(8,128)S(1)}, u32[]{:S(2)}, u32[]{:S(2)}) collective-permute-start(f32[16,256]{1,0:T(8,128)S(1)} %fusion.14), channel_id=1, source_target_pairs={{0,4},{4,0},{8,12},{12,8},{16,20},{20,16},{24,28},{28,24},{1,5},{5... | collective-permute-start | bytes 49160 | tf_op jit(solution)/shard_map/ppermute | solution.py:128
where the time goes:
time: 95.4 us; the launch traced here: 95.3 us
  Pallas kernels  31.4 us (33%)
  starting transfers between devices  31 us (32%)
  waiting for transfers between devices  28.9 us (30%)
  other arithmetic  2.63 us (3%)
  between operations  1.11 us (1%)
    ppermute x24, starting transfers between devices, exchange(): return lax.ppermute(x, axis, [(i, i ^ mask) for i in range(n)])  31 us
    pallas_call x2, Pallas kernels, gradients(): pl.pallas_call(functools.partial(grad_kernel, depth_block=depth_block, gr...  30.5 us
    ppermute x24, waiting for transfers between devices, exchange(): return lax.ppermute(x, axis, [(i, i ^ mask) for i in range(n)])  28.9 us
  transfers between devices with their start and end apart: 24, of which 18 were waited for; matrix products, arithmetic and copies ran while one was open for 2% of the time, Pallas kernels for 1%

commit v1 on v0

--- a/solution.py
+++ b/solution.py
@@ -12,7 +12,7 @@
 step_rate = 48.0
 f32 = jnp.float32
 bf16 = jnp.bfloat16
-VMEM_BYTES = 24 * 1024 * 1024
+VMEM_BYTES = 20 * 1024 * 1024
 
 
 def split(x):
@@ -21,22 +21,21 @@
     return high, low
 
 
-def grad_kernel(obs_hbm, a_ref, b_ref, c_ref, ga_ref, gb_ref, gc_ref,
-                obs, bt_cat, b_cat, at_cat, gbt, sems, *, depth_block, group):
-    depth = c_ref.shape[0]
-    blocks = depth // depth_block
-    n, _ = a_ref.shape
-
-    lanes = obs.shape[-1]
-    panels = obs.shape[1]
+def panel_copy(obs_hbm, dst, sem, block, panel, depth_block):
+    lanes = dst.shape[-1]
+    return pltpu.make_async_copy(
+        obs_hbm.at[:, pl.ds(block * depth_block, depth_block), pl.ds(panel * lanes, lanes)], dst, sem)
+
+
+def grad_kernel(obs_hbm, head_ref, a_ref, b_ref, c_ref, ga_ref, keep_ref, send_ref,
+                obs, bt_cat, b_cat, at_cat, gbt, gb_ref, gc_ref, sems, *, group, cols_own):
+    panels, n, depth_block, lanes = head_ref.shape
+    blocks = c_ref.shape[0] // depth_block
 
     def fetch(g, h):
-        first = pl.multiple_of(g * depth_block, depth_block)
-        return pltpu.make_async_copy(
-            obs_hbm.at[:, pl.ds(first, depth_block), pl.ds(h * lanes, lanes)],
-            obs.at[g, h], sems.at[g, h])
-
-    for g in range(blocks):
+        return panel_copy(obs_hbm, obs.at[g, h], sems.at[g, h], g + 1, h, depth_block)
+
+    for g in range(blocks - 1):
         for h in range(panels):
             fetch(g, h).start()
     b = b_ref[...]
@@ -49,21 +48,26 @@
     ga_ref[...] = jnp.zeros_like(ga_ref)
     gbt[...] = jnp.zeros_like(gbt)
 
-    def block(g, carry):
-        for h in range(panels):
-            fetch(g, h).wait()
-        flat = [obs.at[g, h].reshape(n * depth_block, lanes) for h in range(panels)]
+    def block(g, source):
+        flat = [source.at[h].reshape(n * depth_block, lanes) for h in range(panels)]
         a = a_ref[...]
-        first = pl.multiple_of(g * depth_block, depth_block)
-        ck = c_ref[pl.ds(first, depth_block), :]
+        base = pl.multiple_of(g * depth_block, depth_block)
+        ck = c_ref[pl.ds(base, depth_block), :]
         ckt = ck.T
         rows_c = []
-        for k0 in range(0, depth_block, group):
+
+        def front(k0):
             wide = []
             for k in range(k0, k0 + group):
                 ph, pw = split(a * ck[k:k + 1, :])
                 wide.append(jnp.concatenate([ph, ph, pw], 1))
-            logits = jnp.dot(jnp.concatenate(wide, 0), bt_cat[...], preferred_element_type=f32)
+            return jnp.dot(jnp.concatenate(wide, 0), bt_cat[...], preferred_element_type=f32)
+
+        later = front(0)
+        for k0 in range(0, depth_block, group):
+            logits = later
+            if k0 + group < depth_block:
+                later = front(k0 + group)
             x = jnp.concatenate([
                 jnp.concatenate([p[pl.ds(k, n, stride=depth_block), :] for p in flat], 1)
                 for k in range(k0, k0 + group)], 0)
@@ -89,38 +93,80 @@
                 term = gt * ckt[:, k:k + 1]
                 total = term if total is None else total + term
             gbt[...] += total
-        gc_ref[pl.ds(first, depth_block), :] = jnp.concatenate(rows_c, 0)
+        gc_ref[pl.ds(base, depth_block), :] = jnp.concatenate(rows_c, 0)
+
+    block(0, head_ref)
+
+    def rest(g, carry):
+        for h in range(panels):
+            fetch(g, h).wait()
+        block(g + 1, obs.at[g])
         return carry
 
-    lax.fori_loop(0, blocks, block, 0)
+    lax.fori_loop(0, blocks - 1, rest, 0)
     gb_ref[...] = gbt[...].T
-
-
-def gradients(observed, a, b, c):
+    core = lax.axis_index("row") & 1
+    half_depth = gc_ref.shape[0] // 2
+    half = gb_ref.shape[0] // 2
+    for ref, which in ((keep_ref, core), (send_ref, 1 - core)):
+        for p in range(half // cols_own):
+            start = pl.multiple_of((2 * p + which) * cols_own, cols_own)
+            ref[p * cols_own:(p + 1) * cols_own, :] = gb_ref[pl.ds(start, cols_own), :]
+        start = pl.multiple_of(which * half_depth, half_depth)
+        ref[half:, :] = gc_ref[pl.ds(start, half_depth), :]
+
+
+def gradients(observed, head, a, b, c, cols_own):
     rows, depth, cols = observed.shape
     rank = a.shape[1]
-    depth_block, group, lanes = 8, 2, 128
+    panels, _, depth_block, lanes = head.shape
+    blocks = depth // depth_block
     here = pl.BlockSpec(memory_space=pltpu.VMEM)
     return pl.pallas_call(
-        functools.partial(grad_kernel, depth_block=depth_block, group=group),
-        in_specs=[pl.BlockSpec(memory_space=pltpu.HBM), here, here, here],
+        functools.partial(grad_kernel, group=2, cols_own=cols_own),
+        in_specs=[pl.BlockSpec(memory_space=pltpu.HBM), here, here, here, here],
         out_specs=[here, here, here],
         out_shape=[
             jax.ShapeDtypeStruct((rows, rank), f32),
-            jax.ShapeDtypeStruct((cols, rank), f32),
-            jax.ShapeDtypeStruct((depth, rank), f32),
+            jax.ShapeDtypeStruct(((cols + depth) // 2, rank), f32),
+            jax.ShapeDtypeStruct(((cols + depth) // 2, rank), f32),
         ],
         scratch_shapes=[
-            pltpu.VMEM((depth // depth_block, cols // lanes, rows, depth_block, lanes), jnp.int32),
+            pltpu.VMEM((blocks - 1, panels, rows, depth_block, lanes), jnp.int32),
             pltpu.VMEM((3 * rank, cols), bf16), pltpu.VMEM((3 * cols, rank), bf16),
             pltpu.VMEM((rank, 3 * rows), bf16), pltpu.VMEM((rank, cols), f32),
-            pltpu.SemaphoreType.DMA((depth // depth_block, cols // lanes)),
+            pltpu.VMEM((cols, rank), f32), pltpu.VMEM((depth, rank), f32),
+            pltpu.SemaphoreType.DMA((blocks - 1, panels)),
         ],
         compiler_params=pltpu.CompilerParams(vmem_limit_bytes=VMEM_BYTES),
         cost_estimate=pl.CostEstimate(
             flops=18 * rows * depth * cols * rank, bytes_accessed=4 * rows * depth * cols,
             transcendentals=rows * depth * cols),
-    )(pltpu.with_memory_space_constraint(observed, pltpu.HBM), a, b, c)
+    )(pltpu.with_memory_space_constraint(observed, pltpu.HBM), head, a, b, c)
+
+
+def head_kernel(obs_hbm, head_ref, sems):
+    copies = [
+        panel_copy(obs_hbm, head_ref.at[h], sems.at[h], 0, h, head_ref.shape[2])
+        for h in range(head_ref.shape[0])
+    ]
+    for copy in copies:
+        copy.start()
+    for copy in copies:
+        copy.wait()
+
+
+def first_block(observed, depth_block, lanes):
+    rows, _, cols = observed.shape
+    panels = cols // lanes
+    return pl.pallas_call(
+        head_kernel,
+        in_specs=[pl.BlockSpec(memory_space=pltpu.HBM)],
+        out_specs=pl.BlockSpec(memory_space=pltpu.VMEM),
+        out_shape=jax.ShapeDtypeStruct((panels, rows, depth_block, lanes), observed.dtype),
+        scratch_shapes=[pltpu.SemaphoreType.DMA((panels,))],
+        compiler_params=pltpu.CompilerParams(vmem_limit_bytes=VMEM_BYTES),
+    )(pltpu.with_memory_space_constraint(observed, pltpu.HBM))
 
 
 def exchange(x, axis, mask):
@@ -209,6 +255,7 @@
         return wide.reshape(cols_here, rank), depth
 
     a, b, c = staged(first_factor, second_factor, third_factor)
+    head = first_block(observed, 8, 128)
     c_half = lax.dynamic_slice_in_dim(c, core * half_depth, half_depth, 0)
     held = [b]
     places = [0]
@@ -224,15 +271,10 @@
     wide_b, c = both_cores(b_half, c_half)
     for iteration in range(STEPS):
         last = iteration == STEPS - 1
-        ga, gb, gc = gradients(observed, wide_a, wide_b, c)
+        ga, keep, send = gradients(observed, head, wide_a, wide_b, c, cols_own)
         ga = ga.reshape(col_count, rows_own, rank)
-        gb = gb.reshape(chip_count, 2, cols_own, rank)
-        gc = gc.reshape(2, half_depth, rank)
-        pick = lambda x, axis, which: lax.dynamic_index_in_dim(x, which, axis, keepdims=False)
-        got = exchange(
-            jnp.concatenate([pick(gb, 1, 1 - core).reshape(cols_half, rank), pick(gc, 0, 1 - core)]), "row", 1)
-        gb = pick(gb, 1, core) + got[:cols_half].reshape(chip_count, cols_own, rank)
-        gc = pick(gc, 0, core) + got[cols_half:]
+        both = keep + exchange(send, "row", 1)
+        gb, gc = both[:cols_half], both[cols_half:]
         parts = [jnp.concatenate([take(ga, col), gc])]
         for s in range(1, col_count):
             parts.append(exchange(jnp.concatenate([take(ga, col ^ s), gc]), "col", s))
@@ -240,6 +282,7 @@
         a = a - rate_one * both[:rows_own]
         gc = both[rows_own:]
         if last:
+            gb = gb.reshape(chip_count, cols_own, rank)
             parts = [jnp.concatenate([take(gb, chip), gc])]
             for s in range(1, chip_count):
                 parts.append(exchange(jnp.concatenate([take(gb, chip ^ s), gc]), "row", 2 * s))
@@ -249,7 +292,7 @@
             other = exchange(c_half, "row", 1)
             c = jnp.where(core == 0, jnp.concatenate([c_half, other]), jnp.concatenate([other, c_half]))
         else:
-            both = jnp.concatenate([gb.reshape(cols_half, rank), gc])
+            both = jnp.concatenate([gb, gc])
             for mask in chip_masks:
                 both = both + exchange(both, "row", 2 * mask)
             wide_a = gather_rows(a, a)

time: 95.4 us -> 89.4 us (0.937)
  Pallas kernels: 31.4 us -> 27 us
  waiting for transfers between devices: 28.9 us -> 27.8 us
    pallas_call x2 -> x3, Pallas kernels: 30.5 us -> 26.1 us  [the longest x2 24.5 us: gradients(): pl.pallas_call(functools.partial(grad_kernel, group=2, cols_own=cols_own)...]
    ppermute x24, waiting for transfers between devices: 28.9 us -> 27.8 us  [exchange(): return lax.ppermute(x, axis, [(i, i ^ mask) for i in range(n)])]
  transfers between devices with their start and end apart: 24 -> 24, of which waited for: 18 -> 16; matrix products, arithmetic and copies ran while one was open for 2% -> 2% of each run, Pallas kernels for 1% -> 3%
where the time goes in v1:
time: 89.4 us; the launch traced here: 89.2 us
  starting transfers between devices  30.5 us (34%)
  waiting for transfers between devices  27.8 us (31%)
  Pallas kernels  27 us (30%)
  other arithmetic  2.6 us (3%)
  between operations  1.12 us (1%)
    ppermute x24, starting transfers between devices, exchange(): return lax.ppermute(x, axis, [(i, i ^ mask) for i in range(n)])  30.5 us
    ppermute x24, waiting for transfers between devices, exchange(): return lax.ppermute(x, axis, [(i, i ^ mask) for i in range(n)])  27.8 us
    pallas_call x2, Pallas kernels, gradients(): pl.pallas_call(functools.partial(grad_kernel, group=2, cols_own=cols_own)...  24.5 us
  transfers between devices with their start and end apart: 24, of which 16 were waited for; matrix products, arithmetic and copies ran while one was open for 2% of the time, Pallas kernels for 3%

profile of v1, /device:TPU:0, one launch (start us, length us, event | category | flops | bytes accessed | tf_op | source)
XLA Modules:
  0.0 89.2 jit_solution(3672369547326145756)
XLA Ops:
  0.6 3.0 %collective-permute-start = (f32[64,256]{1,0:T(8,128)}, f32[64,256]{1,0:T(8,128)S(1)}, u32[]{:S(2)}, u32[]{:S(2)}) collective-permute-start(f32[64,256]{1,0:T(8,128)} %a_hbm.1), channel_id=1, source_target_pairs={{0,1},{1,0},{2,3},{3,2},{4,5},{5,4},{6,7},{7,6},{8,9},{9,8},{10,11... | collective-permute-start | bytes 196616 | tf_op jit(solution)/shard_map/ppermute | solution.py:174
  3.7 1.5 %collective-permute-start.1 = (f32[64,256]{1,0:T(8,128)}, f32[64,256]{1,0:T(8,128)S(1)}, u32[]{:S(2)}, u32[]{:S(2)}) collective-permute-start(f32[64,256]{1,0:T(8,128)} %a_hbm.1), channel_id=1, source_target_pairs={{0,2},{1,3},{2,0},{3,1},{4,6},{5,7},{6,4},{7,5},{8,10},{9,11},{10,... | collective-permute-start | bytes 196616 | tf_op jit(solution)/shard_map/ppermute | solution.py:174
  5.2 3.0 %collective-permute-start.3 = (f32[1,32,256]{2,1,0:T(8,128)}, f32[1,32,256]{2,1,0:T(8,128)S(1)}, u32[]{:S(2)}, u32[]{:S(2)}) collective-permute-start(f32[1,32,256]{2,1,0:T(8,128)} %bitcast.148), channel_id=1, source_target_pairs={{0,16},{4,20},{8,24},{12,28},{16,0},{20,4},{24,8},{28,12},{1,17},{... | collective-permute-start | bytes 98312 | tf_op jit(solution)/shard_map/ppermute | solution.py:174
  9.2 1.6 %shard_map.68.head_ref = s32[2,256,8,128]{3,2,1,0:T(8,128)S(1)} custom-call(s32[256,32,256]{2,1,0:T(8,128)} %obs_hbm.5), custom_call_target="tpu_custom_call" | custom-call | tf_op jit(solution)/shard_map/pallas_call | solution.py:162
  10.8 1.6 %collective-permute-start.4 = (f32[2,32,256]{2,1,0:T(8,128)S(1)}, f32[2,32,256]{2,1,0:T(8,128)S(1)}, u32[]{:S(2)}, u32[]{:S(2)}) collective-permute-start(f32[2,32,256]{2,1,0:T(8,128)S(1)} %pad_maximum_fusion.24), channel_id=1, source_target_pairs={{0,8},{4,12},{8,0},{12,4},{16,24},{20,28},{24,16},{28,20},{1,9},{5... | collective-permute-start | bytes 196616 | tf_op jit(solution)/shard_map/ppermute | solution.py:174
  12.6 2.5 %collective-permute-done.4 = f32[2,32,256]{2,1,0:T(8,128)S(1)} collective-permute-done((f32[2,32,256]{2,1,0:T(8,128)S(1)}, f32[2,32,256]{2,1,0:T(8,128)S(1)}, u32[]{:S(2)}, u32[]{:S(2)}) %collective-permute-start.4) | collective-permute-done | bytes 65568 | tf_op jit(solution)/shard_map/ppermute | solution.py:174
  16.8 12.3 %shard_map.69 = (f32[256,256]{1,0:T(8,128)S(1)}, f32[144,256]{1,0:T(8,128)S(1)}, f32[144,256]{1,0:T(8,128)S(1)}) custom-call(s32[256,32,256]{2,1,0:T(8,128)} %obs_hbm.5, s32[2,256,8,128]{3,2,1,0:T(8,128)S(1)} %shard_map.68.head_ref, f32[256,256]{1,0:T(8,128)S(1)} %fusion.1.a_ref, f32[256,256]{1,0:T(8,128)S(1)} %bitcast.121, ...), custom_call_target="tpu_custom_call" | custom-call | flops 9663676416 | bytes 8388608 | tf_op jit(solution)/shard_map/pallas_call | solution.py:125
  30.6 1.6 %collective-permute-start.7 = (f32[80,256]{1,0:T(8,128)S(1)}, f32[80,256]{1,0:T(8,128)S(1)}, u32[]{:S(2)}, u32[]{:S(2)}) collective-permute-start(f32[80,256]{1,0:T(8,128)S(1)} %get-tuple-element.64), channel_id=1, source_target_pairs={{0,1},{1,0},{2,3},{3,2},{4,5},{5,4},{6,7},{7,6},{8,9},{9,8},{10,11... | collective-permute-start | bytes 245768 | tf_op jit(solution)/shard_map/ppermute | solution.py:174
  32.2 1.5 %collective-permute-start.8 = (f32[80,256]{1,0:T(8,128)S(1)}, f32[80,256]{1,0:T(8,128)S(1)}, u32[]{:S(2)}, u32[]{:S(2)}) collective-permute-start(f32[80,256]{1,0:T(8,128)S(1)} %get-tuple-element.65), channel_id=1, source_target_pairs={{0,2},{1,3},{2,0},{3,1},{4,6},{5,7},{6,4},{7,5},{8,10},{9,11},{10,... | collective-permute-start | bytes 245768 | tf_op jit(solution)/shard_map/ppermute | solution.py:174
  35.2 2.3 %collective-permute-done.8 = f32[80,256]{1,0:T(8,128)S(1)} collective-permute-done((f32[80,256]{1,0:T(8,128)S(1)}, f32[80,256]{1,0:T(8,128)S(1)}, u32[]{:S(2)}, u32[]{:S(2)}) %collective-permute-start.8) | collective-permute-done | bytes 81952 | tf_op jit(solution)/shard_map/ppermute | solution.py:174
  37.5 1.6 %collective-permute-done.9 = f32[80,256]{1,0:T(8,128)S(1)} collective-permute-done((f32[80,256]{1,0:T(8,128)S(1)}, f32[80,256]{1,0:T(8,128)S(1)}, u32[]{:S(2)}, u32[]{:S(2)}) %collective-permute-start.9) | collective-permute-done | bytes 81952 | tf_op jit(solution)/shard_map/ppermute | solution.py:174
  40.6 2.1 %collective-permute-start.12 = (f32[64,256]{1,0:T(8,128)S(1)}, f32[64,256]{1,0:T(8,128)S(1)}, u32[]{:S(2)}, u32[]{:S(2)}) collective-permute-start(f32[64,256]{1,0:T(8,128)S(1)} %fusion.9), channel_id=1, source_target_pairs={{0,3},{1,2},{2,1},{3,0},{4,7},{5,6},{6,5},{7,4},{8,11},{9,10},{10,... | collective-permute-start | bytes 196616 | tf_op jit(solution)/shard_map/ppermute | solution.py:174
  42.7 1.6 %collective-permute-start.13 = (f32[144,256]{1,0:T(8,128)S(1)}, f32[144,256]{1,0:T(8,128)S(1)}, u32[]{:S(2)}, u32[]{:S(2)}) collective-permute-start(f32[144,256]{1,0:T(8,128)S(1)} %pad_maximum_fusion.15), channel_id=1, source_target_pairs={{0,8},{4,12},{8,0},{12,4},{16,24},{20,28},{24,16},{28,20},{1,9},{5... | collective-permute-start | bytes 442376 | tf_op jit(solution)/shard_map/ppermute | solution.py:174
  44.3 1.4 %collective-permute-done.12 = f32[64,256]{1,0:T(8,128)S(1)} collective-permute-done((f32[64,256]{1,0:T(8,128)S(1)}, f32[64,256]{1,0:T(8,128)S(1)}, u32[]{:S(2)}, u32[]{:S(2)}) %collective-permute-start.12) | collective-permute-done | bytes 65568 | tf_op jit(solution)/shard_map/ppermute | solution.py:174
  45.9 2.0 %collective-permute-done.13 = f32[144,256]{1,0:T(8,128)S(1)} collective-permute-done((f32[144,256]{1,0:T(8,128)S(1)}, f32[144,256]{1,0:T(8,128)S(1)}, u32[]{:S(2)}, u32[]{:S(2)}) %collective-permute-start.13) | collective-permute-done | bytes 147488 | tf_op jit(solution)/shard_map/ppermute | solution.py:174
  47.9 3.8 %collective-permute-start.14 = (f32[144,256]{1,0:T(8,128)S(1)}, f32[144,256]{1,0:T(8,128)S(1)}, u32[]{:S(2)}, u32[]{:S(2)}) collective-permute-start(f32[144,256]{1,0:T(8,128)S(1)} %fusion.17), channel_id=1, source_target_pairs={{0,24},{4,28},{8,16},{12,20},{16,8},{20,12},{24,0},{28,4},{1,25},{... | collective-permute-start | bytes 442376 | tf_op jit(solution)/shard_map/ppermute | solution.py:174
  51.7 3.3 %collective-permute-done.14 = f32[144,256]{1,0:T(8,128)S(1)} collective-permute-done((f32[144,256]{1,0:T(8,128)S(1)}, f32[144,256]{1,0:T(8,128)S(1)}, u32[]{:S(2)}, u32[]{:S(2)}) %collective-permute-start.14) | collective-permute-done | bytes 147488 | tf_op jit(solution)/shard_map/ppermute | solution.py:174
  56.6 12.2 %shard_map.70 = (f32[256,256]{1,0:T(8,128)S(1)}, f32[144,256]{1,0:T(8,128)S(1)}, f32[144,256]{1,0:T(8,128)S(1)}) custom-call(s32[256,32,256]{2,1,0:T(8,128)} %obs_hbm.5, s32[2,256,8,128]{3,2,1,0:T(8,128)S(1)} %shard_map.68.head_ref, f32[256,256]{1,0:T(8,128)S(1)} %fusion.a_ref, f32[256,256]{1,0:T(8,128)S(1)} %bitcast.120, ...), custom_call_target="tpu_custom_call" | custom-call | flops 9663676416 | bytes 8388608 | tf_op jit(solution)/shard_map/pallas_call | solution.py:125
  71.8 2.1 %collective-permute-start.19 = (f32[80,256]{1,0:T(8,128)S(1)}, f32[80,256]{1,0:T(8,128)S(1)}, u32[]{:S(2)}, u32[]{:S(2)}) collective-permute-start(f32[80,256]{1,0:T(8,128)S(1)} %get-tuple-element.60), channel_id=1, source_target_pairs={{0,3},{1,2},{2,1},{3,0},{4,7},{5,6},{6,5},{7,4},{8,11},{9,10},{10,... | collective-permute-start | bytes 245768 | tf_op jit(solution)/shard_map/ppermute | solution.py:174
  75.2 2.0 %collective-permute-done.18 = f32[80,256]{1,0:T(8,128)S(1)} collective-permute-done((f32[80,256]{1,0:T(8,128)S(1)}, f32[80,256]{1,0:T(8,128)S(1)}, u32[]{:S(2)}, u32[]{:S(2)}) %collective-permute-start.18) | collective-permute-done | bytes 81952 | tf_op jit(solution)/shard_map/ppermute | solution.py:174
  77.2 1.6 %collective-permute-start.20 = (f32[48,256]{1,0:T(8,128)S(1)}, f32[48,256]{1,0:T(8,128)S(1)}, u32[]{:S(2)}, u32[]{:S(2)}) collective-permute-start(f32[48,256]{1,0:T(8,128)S(1)} %get-tuple-element.58), channel_id=1, source_target_pairs={{0,8},{4,12},{8,0},{12,4},{16,24},{20,28},{24,16},{28,20},{1,9},{5... | collective-permute-start | bytes 147464 | tf_op jit(solution)/shard_map/ppermute | solution.py:174
  78.8 2.6 %collective-permute-start.21 = (f32[48,256]{1,0:T(8,128)S(1)}, f32[48,256]{1,0:T(8,128)S(1)}, u32[]{:S(2)}, u32[]{:S(2)}) collective-permute-start(f32[48,256]{1,0:T(8,128)S(1)} %get-tuple-element.59), channel_id=1, source_target_pairs={{0,16},{4,20},{8,24},{12,28},{16,0},{20,4},{24,8},{28,12},{1,17},{... | collective-permute-start | bytes 147464 | tf_op jit(solution)/shard_map/ppermute | solution.py:174
  82.4 3.0 %collective-permute-done.21 = f32[48,256]{1,0:T(8,128)S(1)} collective-permute-done((f32[48,256]{1,0:T(8,128)S(1)}, f32[48,256]{1,0:T(8,128)S(1)}, u32[]{:S(2)}, u32[]{:S(2)}) %collective-permute-start.21) | collective-permute-done | bytes 49184 | tf_op jit(solution)/shard_map/ppermute | solution.py:174
  85.4 1.9 %collective-permute-done.22 = f32[48,256]{1,0:T(8,128)S(1)} collective-permute-done((f32[48,256]{1,0:T(8,128)S(1)}, f32[48,256]{1,0:T(8,128)S(1)}, u32[]{:S(2)}, u32[]{:S(2)}) %collective-permute-start.22) | collective-permute-done | bytes 49184 | tf_op jit(solution)/shard_map/ppermute | solution.py:174
  (92 shorter events, 15.9 us)
Async XLA Ops:
  0.6 11.8 %collective-permute-start = (f32[64,256]{1,0:T(8,128)}, f32[64,256]{1,0:T(8,128)S(1)}, u32[]{:S(2)}, u32[]{:S(2)}) collective-permute-start(f32[64,256]{1,0:T(8,128)} %a_hbm.1), channel_id=1, source_target_pairs={{0,1},{1,0},{2,3},{3,2},{4,5},{5,4},{6,7},{7,6},{8,9},{9,8},{10,11... | collective-permute-start | bytes 196616 | tf_op jit(solution)/shard_map/ppermute | solution.py:174
  3.7 8.8 %collective-permute-start.1 = (f32[64,256]{1,0:T(8,128)}, f32[64,256]{1,0:T(8,128)S(1)}, u32[]{:S(2)}, u32[]{:S(2)}) collective-permute-start(f32[64,256]{1,0:T(8,128)} %a_hbm.1), channel_id=1, source_target_pairs={{0,2},{1,3},{2,0},{3,1},{4,6},{5,7},{6,4},{7,5},{8,10},{9,11},{10,... | collective-permute-start | bytes 196616 | tf_op jit(solution)/shard_map/ppermute | solution.py:174
  5.2 7.2 %collective-permute-start.2 = (f32[64,256]{1,0:T(8,128)}, f32[64,256]{1,0:T(8,128)S(1)}, u32[]{:S(2)}, u32[]{:S(2)}) collective-permute-start(f32[64,256]{1,0:T(8,128)} %a_hbm.1), channel_id=1, source_target_pairs={{0,3},{1,2},{2,1},{3,0},{4,7},{5,6},{6,5},{7,4},{8,11},{9,10},{10,... | collective-permute-start | bytes 196616 | tf_op jit(solution)/shard_map/ppermute | solution.py:174
  5.2 5.6 %collective-permute-start.3 = (f32[1,32,256]{2,1,0:T(8,128)}, f32[1,32,256]{2,1,0:T(8,128)S(1)}, u32[]{:S(2)}, u32[]{:S(2)}) collective-permute-start(f32[1,32,256]{2,1,0:T(8,128)} %bitcast.148), channel_id=1, source_target_pairs={{0,16},{4,20},{8,24},{12,28},{16,0},{20,4},{24,8},{28,12},{1,17},{... | collective-permute-start | bytes 98312 | tf_op jit(solution)/shard_map/ppermute | solution.py:174
  10.8 4.3 %collective-permute-start.4 = (f32[2,32,256]{2,1,0:T(8,128)S(1)}, f32[2,32,256]{2,1,0:T(8,128)S(1)}, u32[]{:S(2)}, u32[]{:S(2)}) collective-permute-start(f32[2,32,256]{2,1,0:T(8,128)S(1)} %pad_maximum_fusion.24), channel_id=1, source_target_pairs={{0,8},{4,12},{8,0},{12,4},{16,24},{20,28},{24,16},{28,20},{1,9},{5... | collective-permute-start | bytes 196616 | tf_op jit(solution)/shard_map/ppermute | solution.py:174
  15.3 1.4 %collective-permute-start.5 = (f32[144,256]{1,0:T(8,128)S(1)}, f32[144,256]{1,0:T(8,128)S(1)}, u32[]{:S(2)}, u32[]{:S(2)}) collective-permute-start(f32[144,256]{1,0:T(8,128)S(1)} %pad_maximum_fusion.14), channel_id=1, source_target_pairs={{0,4},{4,0},{8,12},{12,8},{16,20},{20,16},{24,28},{28,24},{1,5},{5... | collective-permute-start | bytes 442376 | tf_op jit(solution)/shard_map/ppermute | solution.py:174
  29.1 1.4 %collective-permute-start.6 = (f32[144,256]{1,0:T(8,128)S(1)}, f32[144,256]{1,0:T(8,128)S(1)}, u32[]{:S(2)}, u32[]{:S(2)}) collective-permute-start(f32[144,256]{1,0:T(8,128)S(1)} %get-tuple-element.17), channel_id=1, source_target_pairs={{0,4},{4,0},{8,12},{12,8},{16,20},{20,16},{24,28},{28,24},{1,5},{5... | collective-permute-start | bytes 442376 | tf_op jit(solution)/shard_map/ppermute | solution.py:174
  30.6 4.6 %collective-permute-start.7 = (f32[80,256]{1,0:T(8,128)S(1)}, f32[80,256]{1,0:T(8,128)S(1)}, u32[]{:S(2)}, u32[]{:S(2)}) collective-permute-start(f32[80,256]{1,0:T(8,128)S(1)} %get-tuple-element.64), channel_id=1, source_target_pairs={{0,1},{1,0},{2,3},{3,2},{4,5},{5,4},{6,7},{7,6},{8,9},{9,8},{10,11... | collective-permute-start | bytes 245768 | tf_op jit(solution)/shard_map/ppermute | solution.py:174
  32.2 5.3 %collective-permute-start.8 = (f32[80,256]{1,0:T(8,128)S(1)}, f32[80,256]{1,0:T(8,128)S(1)}, u32[]{:S(2)}, u32[]{:S(2)}) collective-permute-start(f32[80,256]{1,0:T(8,128)S(1)} %get-tuple-element.65), channel_id=1, source_target_pairs={{0,2},{1,3},{2,0},{3,1},{4,6},{5,7},{6,4},{7,5},{8,10},{9,11},{10,... | collective-permute-start | bytes 245768 | tf_op jit(solution)/shard_map/ppermute | solution.py:174
  33.7 5.3 %collective-permute-start.9 = (f32[80,256]{1,0:T(8,128)S(1)}, f32[80,256]{1,0:T(8,128)S(1)}, u32[]{:S(2)}, u32[]{:S(2)}) collective-permute-start(f32[80,256]{1,0:T(8,128)S(1)} %get-tuple-element.63), channel_id=1, source_target_pairs={{0,3},{1,2},{2,1},{3,0},{4,7},{5,6},{6,5},{7,4},{8,11},{9,10},{10,... | collective-permute-start | bytes 245768 | tf_op jit(solution)/shard_map/ppermute | solution.py:174
  39.1 5.2 %collective-permute-start.10 = (f32[64,256]{1,0:T(8,128)S(1)}, f32[64,256]{1,0:T(8,128)S(1)}, u32[]{:S(2)}, u32[]{:S(2)}) collective-permute-start(f32[64,256]{1,0:T(8,128)S(1)} %fusion.9), channel_id=1, source_target_pairs={{0,1},{1,0},{2,3},{3,2},{4,5},{5,4},{6,7},{7,6},{8,9},{9,8},{10,11... | collective-permute-start | bytes 196616 | tf_op jit(solution)/shard_map/ppermute | solution.py:174
  39.7 4.6 %collective-permute-start.11 = (f32[64,256]{1,0:T(8,128)S(1)}, f32[64,256]{1,0:T(8,128)S(1)}, u32[]{:S(2)}, u32[]{:S(2)}) collective-permute-start(f32[64,256]{1,0:T(8,128)S(1)} %fusion.9), channel_id=1, source_target_pairs={{0,2},{1,3},{2,0},{3,1},{4,6},{5,7},{6,4},{7,5},{8,10},{9,11},{10,... | collective-permute-start | bytes 196616 | tf_op jit(solution)/shard_map/ppermute | solution.py:174
  40.6 5.2 %collective-permute-start.12 = (f32[64,256]{1,0:T(8,128)S(1)}, f32[64,256]{1,0:T(8,128)S(1)}, u32[]{:S(2)}, u32[]{:S(2)}) collective-permute-start(f32[64,256]{1,0:T(8,128)S(1)} %fusion.9), channel_id=1, source_target_pairs={{0,3},{1,2},{2,1},{3,0},{4,7},{5,6},{6,5},{7,4},{8,11},{9,10},{10,... | collective-permute-start | bytes 196616 | tf_op jit(solution)/shard_map/ppermute | solution.py:174
  42.7 5.2 %collective-permute-start.13 = (f32[144,256]{1,0:T(8,128)S(1)}, f32[144,256]{1,0:T(8,128)S(1)}, u32[]{:S(2)}, u32[]{:S(2)}) collective-permute-start(f32[144,256]{1,0:T(8,128)S(1)} %pad_maximum_fusion.15), channel_id=1, source_target_pairs={{0,8},{4,12},{8,0},{12,4},{16,24},{20,28},{24,16},{28,20},{1,9},{5... | collective-permute-start | bytes 442376 | tf_op jit(solution)/shard_map/ppermute | solution.py:174
  47.9 7.1 %collective-permute-start.14 = (f32[144,256]{1,0:T(8,128)S(1)}, f32[144,256]{1,0:T(8,128)S(1)}, u32[]{:S(2)}, u32[]{:S(2)}) collective-permute-start(f32[144,256]{1,0:T(8,128)S(1)} %fusion.17), channel_id=1, source_target_pairs={{0,24},{4,28},{8,16},{12,20},{16,8},{20,12},{24,0},{28,4},{1,25},{... | collective-permute-start | bytes 442376 | tf_op jit(solution)/shard_map/ppermute | solution.py:174
  55.1 1.4 %collective-permute-start.15 = (f32[144,256]{1,0:T(8,128)S(1)}, f32[144,256]{1,0:T(8,128)S(1)}, u32[]{:S(2)}, u32[]{:S(2)}) collective-permute-start(f32[144,256]{1,0:T(8,128)S(1)} %pad_maximum_fusion.16), channel_id=1, source_target_pairs={{0,4},{4,0},{8,12},{12,8},{16,20},{20,16},{24,28},{28,24},{1,5},{5... | collective-permute-start | bytes 442376 | tf_op jit(solution)/shard_map/ppermute | solution.py:174
  68.8 1.4 %collective-permute-start.16 = (f32[144,256]{1,0:T(8,128)S(1)}, f32[144,256]{1,0:T(8,128)S(1)}, u32[]{:S(2)}, u32[]{:S(2)}) collective-permute-start(f32[144,256]{1,0:T(8,128)S(1)} %get-tuple-element.20), channel_id=1, source_target_pairs={{0,4},{4,0},{8,12},{12,8},{16,20},{20,16},{24,28},{28,24},{1,5},{5... | collective-permute-start | bytes 442376 | tf_op jit(solution)/shard_map/ppermute | solution.py:174
  70.3 4.9 %collective-permute-start.17 = (f32[80,256]{1,0:T(8,128)S(1)}, f32[80,256]{1,0:T(8,128)S(1)}, u32[]{:S(2)}, u32[]{:S(2)}) collective-permute-start(f32[80,256]{1,0:T(8,128)S(1)} %get-tuple-element.61), channel_id=1, source_target_pairs={{0,1},{1,0},{2,3},{3,2},{4,5},{5,4},{6,7},{7,6},{8,9},{9,8},{10,11... | collective-permute-start | bytes 245768 | tf_op jit(solution)/shard_map/ppermute | solution.py:174
  71.0 6.2 %collective-permute-start.18 = (f32[80,256]{1,0:T(8,128)S(1)}, f32[80,256]{1,0:T(8,128)S(1)}, u32[]{:S(2)}, u32[]{:S(2)}) collective-permute-start(f32[80,256]{1,0:T(8,128)S(1)} %get-tuple-element.62), channel_id=1, source_target_pairs={{0,2},{1,3},{2,0},{3,1},{4,6},{5,7},{6,4},{7,5},{8,10},{9,11},{10,... | collective-permute-start | bytes 245768 | tf_op jit(solution)/shard_map/ppermute | solution.py:174
  71.8 5.4 %collective-permute-start.19 = (f32[80,256]{1,0:T(8,128)S(1)}, f32[80,256]{1,0:T(8,128)S(1)}, u32[]{:S(2)}, u32[]{:S(2)}) collective-permute-start(f32[80,256]{1,0:T(8,128)S(1)} %get-tuple-element.60), channel_id=1, source_target_pairs={{0,3},{1,2},{2,1},{3,0},{4,7},{5,6},{6,5},{7,4},{8,11},{9,10},{10,... | collective-permute-start | bytes 245768 | tf_op jit(solution)/shard_map/ppermute | solution.py:174
  77.2 5.2 %collective-permute-start.20 = (f32[48,256]{1,0:T(8,128)S(1)}, f32[48,256]{1,0:T(8,128)S(1)}, u32[]{:S(2)}, u32[]{:S(2)}) collective-permute-start(f32[48,256]{1,0:T(8,128)S(1)} %get-tuple-element.58), channel_id=1, source_target_pairs={{0,8},{4,12},{8,0},{12,4},{16,24},{20,28},{24,16},{28,20},{1,9},{5... | collective-permute-start | bytes 147464 | tf_op jit(solution)/shard_map/ppermute | solution.py:174
  78.8 6.6 %collective-permute-start.21 = (f32[48,256]{1,0:T(8,128)S(1)}, f32[48,256]{1,0:T(8,128)S(1)}, u32[]{:S(2)}, u32[]{:S(2)}) collective-permute-start(f32[48,256]{1,0:T(8,128)S(1)} %get-tuple-element.59), channel_id=1, source_target_pairs={{0,16},{4,20},{8,24},{12,28},{16,0},{20,4},{24,8},{28,12},{1,17},{... | collective-permute-start | bytes 147464 | tf_op jit(solution)/shard_map/ppermute | solution.py:174
  81.4 5.9 %collective-permute-start.22 = (f32[48,256]{1,0:T(8,128)S(1)}, f32[48,256]{1,0:T(8,128)S(1)}, u32[]{:S(2)}, u32[]{:S(2)}) collective-permute-start(f32[48,256]{1,0:T(8,128)S(1)} %get-tuple-element.57), channel_id=1, source_target_pairs={{0,24},{4,28},{8,16},{12,20},{16,8},{20,12},{24,0},{28,4},{1,25},{... | collective-permute-start | bytes 147464 | tf_op jit(solution)/shard_map/ppermute | solution.py:174
  87.3 1.2 %collective-permute-start.23 = (f32[16,256]{1,0:T(8,128)S(1)}, f32[16,256]{1,0:T(8,128)S(1)}, u32[]{:S(2)}, u32[]{:S(2)}) collective-permute-start(f32[16,256]{1,0:T(8,128)S(1)} %fusion.14), channel_id=1, source_target_pairs={{0,4},{4,0},{8,12},{12,8},{16,20},{20,16},{24,28},{28,24},{1,5},{5... | collective-permute-start | bytes 49160 | tf_op jit(solution)/shard_map/ppermute | solution.py:174
  (2 other events, 31.9 us)

commit v2 on v1

--- a/solution.py
+++ b/solution.py
@@ -28,7 +28,7 @@
 
 
 def grad_kernel(obs_hbm, head_ref, a_ref, b_ref, c_ref, ga_ref, keep_ref, send_ref,
-                obs, bt_cat, b_cat, at_cat, gbt, gb_ref, gc_ref, sems, *, group, cols_own):
+                obs, bt_cat, b_cat, at_cat, gbt, gb_ref, gc_ref, ahead, sems, *, group, cols_own):
     panels, n, depth_block, lanes = head_ref.shape
     blocks = c_ref.shape[0] // depth_block
 
@@ -48,7 +48,14 @@
     ga_ref[...] = jnp.zeros_like(ga_ref)
     gbt[...] = jnp.zeros_like(gbt)
 
-    def block(g, source):
+    def front(rows):
+        wide = []
+        for k in range(group):
+            ph, pw = split(a_ref[...] * rows[k:k + 1, :])
+            wide.append(jnp.concatenate([ph, ph, pw], 1))
+        return jnp.dot(jnp.concatenate(wide, 0), bt_cat[...], preferred_element_type=f32)
+
+    def block(g, source, more=True):
         flat = [source.at[h].reshape(n * depth_block, lanes) for h in range(panels)]
         a = a_ref[...]
         base = pl.multiple_of(g * depth_block, depth_block)
@@ -56,18 +63,15 @@
         ckt = ck.T
         rows_c = []
 
-        def front(k0):
-            wide = []
-            for k in range(k0, k0 + group):
-                ph, pw = split(a * ck[k:k + 1, :])
-                wide.append(jnp.concatenate([ph, ph, pw], 1))
-            return jnp.dot(jnp.concatenate(wide, 0), bt_cat[...], preferred_element_type=f32)
-
-        later = front(0)
+        if more:
+            following = c_ref[pl.ds(pl.multiple_of(base + depth_block, depth_block), depth_block), :]
+        later = ahead[...]
         for k0 in range(0, depth_block, group):
             logits = later
             if k0 + group < depth_block:
-                later = front(k0 + group)
+                later = front(ck[k0 + group:k0 + 2 * group])
+            elif more:
+                ahead[...] = front(following[:group])
             x = jnp.concatenate([
                 jnp.concatenate([p[pl.ds(k, n, stride=depth_block), :] for p in flat], 1)
                 for k in range(k0, k0 + group)], 0)
@@ -95,15 +99,18 @@
             gbt[...] += total
         gc_ref[pl.ds(base, depth_block), :] = jnp.concatenate(rows_c, 0)
 
-    block(0, head_ref)
-
     def rest(g, carry):
         for h in range(panels):
             fetch(g, h).wait()
         block(g + 1, obs.at[g])
         return carry
 
-    lax.fori_loop(0, blocks - 1, rest, 0)
+    ahead[...] = front(c_ref[:group, :])
+    block(0, head_ref)
+    lax.fori_loop(0, blocks - 2, rest, 0)
+    for h in range(panels):
+        fetch(blocks - 2, h).wait()
+    block(blocks - 1, obs.at[blocks - 2], more=False)
     gb_ref[...] = gbt[...].T
     core = lax.axis_index("row") & 1
     half_depth = gc_ref.shape[0] // 2
@@ -121,9 +128,10 @@
     rank = a.shape[1]
     panels, _, depth_block, lanes = head.shape
     blocks = depth // depth_block
+    group = 1
     here = pl.BlockSpec(memory_space=pltpu.VMEM)
     return pl.pallas_call(
-        functools.partial(grad_kernel, group=2, cols_own=cols_own),
+        functools.partial(grad_kernel, group=group, cols_own=cols_own),
         in_specs=[pl.BlockSpec(memory_space=pltpu.HBM), here, here, here, here],
         out_specs=[here, here, here],
         out_shape=[
@@ -136,6 +144,7 @@
             pltpu.VMEM((3 * rank, cols), bf16), pltpu.VMEM((3 * cols, rank), bf16),
             pltpu.VMEM((rank, 3 * rows), bf16), pltpu.VMEM((rank, cols), f32),
             pltpu.VMEM((cols, rank), f32), pltpu.VMEM((depth, rank), f32),
+            pltpu.VMEM((group * rows, cols), f32),
             pltpu.SemaphoreType.DMA((blocks - 1, panels)),
         ],
         compiler_params=pltpu.CompilerParams(vmem_limit_bytes=VMEM_BYTES),

time: 89.4 us -> 89.2 us (level)
  transfers between devices with their start and end apart: 24 -> 24, of which waited for: 16 -> 17; matrix products, arithmetic and copies ran while one was open for 2% -> 2% of each run, Pallas kernels for 3% -> 3%
where the time goes in v2:
time: 89.2 us; the launch traced here: 89 us
  starting transfers between devices  30.5 us (34%)
  waiting for transfers between devices  27.8 us (31%)
  Pallas kernels  26.8 us (30%)
  other arithmetic  2.6 us (3%)
  between operations  1.11 us (1%)
    ppermute x24, starting transfers between devices, exchange(): return lax.ppermute(x, axis, [(i, i ^ mask) for i in range(n)])  30.5 us
    ppermute x24, waiting for transfers between devices, exchange(): return lax.ppermute(x, axis, [(i, i ^ mask) for i in range(n)])  27.8 us
    pallas_call x2, Pallas kernels, gradients(): pl.pallas_call(functools.partial(grad_kernel, group=group, cols_own=cols_...  24.4 us
  transfers between devices with their start and end apart: 24, of which 17 were waited for; matrix products, arithmetic and copies ran while one was open for 2% of the time, Pallas kernels for 3%

profile of v2, /device:TPU:0, one launch (start us, length us, event | category | flops | bytes accessed | tf_op | source)
XLA Modules:
  0.0 89.0 jit_solution(3094344295665740540)
XLA Ops:
  0.6 3.0 %collective-permute-start = (f32[64,256]{1,0:T(8,128)}, f32[64,256]{1,0:T(8,128)S(1)}, u32[]{:S(2)}, u32[]{:S(2)}) collective-permute-start(f32[64,256]{1,0:T(8,128)} %a_hbm.1), channel_id=1, source_target_pairs={{0,1},{1,0},{2,3},{3,2},{4,5},{5,4},{6,7},{7,6},{8,9},{9,8},{10,11... | collective-permute-start | bytes 196616 | tf_op jit(solution)/shard_map/ppermute | solution.py:183
  3.7 1.5 %collective-permute-start.1 = (f32[64,256]{1,0:T(8,128)}, f32[64,256]{1,0:T(8,128)S(1)}, u32[]{:S(2)}, u32[]{:S(2)}) collective-permute-start(f32[64,256]{1,0:T(8,128)} %a_hbm.1), channel_id=1, source_target_pairs={{0,2},{1,3},{2,0},{3,1},{4,6},{5,7},{6,4},{7,5},{8,10},{9,11},{10,... | collective-permute-start | bytes 196616 | tf_op jit(solution)/shard_map/ppermute | solution.py:183
  5.2 3.0 %collective-permute-start.3 = (f32[1,32,256]{2,1,0:T(8,128)}, f32[1,32,256]{2,1,0:T(8,128)S(1)}, u32[]{:S(2)}, u32[]{:S(2)}) collective-permute-start(f32[1,32,256]{2,1,0:T(8,128)} %bitcast.148), channel_id=1, source_target_pairs={{0,16},{4,20},{8,24},{12,28},{16,0},{20,4},{24,8},{28,12},{1,17},{... | collective-permute-start | bytes 98312 | tf_op jit(solution)/shard_map/ppermute | solution.py:183
  9.2 1.6 %shard_map.68.head_ref = s32[2,256,8,128]{3,2,1,0:T(8,128)S(1)} custom-call(s32[256,32,256]{2,1,0:T(8,128)} %obs_hbm.5), custom_call_target="tpu_custom_call" | custom-call | tf_op jit(solution)/shard_map/pallas_call | solution.py:171
  10.8 1.6 %collective-permute-start.4 = (f32[2,32,256]{2,1,0:T(8,128)S(1)}, f32[2,32,256]{2,1,0:T(8,128)S(1)}, u32[]{:S(2)}, u32[]{:S(2)}) collective-permute-start(f32[2,32,256]{2,1,0:T(8,128)S(1)} %pad_maximum_fusion.24), channel_id=1, source_target_pairs={{0,8},{4,12},{8,0},{12,4},{16,24},{20,28},{24,16},{28,20},{1,9},{5... | collective-permute-start | bytes 196616 | tf_op jit(solution)/shard_map/ppermute | solution.py:183
  12.6 2.5 %collective-permute-done.4 = f32[2,32,256]{2,1,0:T(8,128)S(1)} collective-permute-done((f32[2,32,256]{2,1,0:T(8,128)S(1)}, f32[2,32,256]{2,1,0:T(8,128)S(1)}, u32[]{:S(2)}, u32[]{:S(2)}) %collective-permute-start.4) | collective-permute-done | bytes 65568 | tf_op jit(solution)/shard_map/ppermute | solution.py:183
  15.4 1.3 %collective-permute-done.5 = f32[144,256]{1,0:T(8,128)S(1)} collective-permute-done((f32[144,256]{1,0:T(8,128)S(1)}, f32[144,256]{1,0:T(8,128)S(1)}, u32[]{:S(2)}, u32[]{:S(2)}) %collective-permute-start.5) | collective-permute-done | bytes 147488 | tf_op jit(solution)/shard_map/ppermute | solution.py:183
  16.8 12.2 %shard_map.69 = (f32[256,256]{1,0:T(8,128)S(1)}, f32[144,256]{1,0:T(8,128)S(1)}, f32[144,256]{1,0:T(8,128)S(1)}) custom-call(s32[256,32,256]{2,1,0:T(8,128)} %obs_hbm.5, s32[2,256,8,128]{3,2,1,0:T(8,128)S(1)} %shard_map.68.head_ref, f32[256,256]{1,0:T(8,128)S(1)} %fusion.1.a_ref, f32[256,256]{1,0:T(8,128)S(1)} %bitcast.121, ...), custom_call_target="tpu_custom_call" | custom-call | flops 9663676416 | bytes 8388608 | tf_op jit(solution)/shard_map/pallas_call | solution.py:133
  30.5 1.6 %collective-permute-start.7 = (f32[80,256]{1,0:T(8,128)S(1)}, f32[80,256]{1,0:T(8,128)S(1)}, u32[]{:S(2)}, u32[]{:S(2)}) collective-permute-start(f32[80,256]{1,0:T(8,128)S(1)} %get-tuple-element.64), channel_id=1, source_target_pairs={{0,1},{1,0},{2,3},{3,2},{4,5},{5,4},{6,7},{7,6},{8,9},{9,8},{10,11... | collective-permute-start | bytes 245768 | tf_op jit(solution)/shard_map/ppermute | solution.py:183
  32.0 1.5 %collective-permute-start.8 = (f32[80,256]{1,0:T(8,128)S(1)}, f32[80,256]{1,0:T(8,128)S(1)}, u32[]{:S(2)}, u32[]{:S(2)}) collective-permute-start(f32[80,256]{1,0:T(8,128)S(1)} %get-tuple-element.65), channel_id=1, source_target_pairs={{0,2},{1,3},{2,0},{3,1},{4,6},{5,7},{6,4},{7,5},{8,10},{9,11},{10,... | collective-permute-start | bytes 245768 | tf_op jit(solution)/shard_map/ppermute | solution.py:183
  35.0 2.3 %collective-permute-done.8 = f32[80,256]{1,0:T(8,128)S(1)} collective-permute-done((f32[80,256]{1,0:T(8,128)S(1)}, f32[80,256]{1,0:T(8,128)S(1)}, u32[]{:S(2)}, u32[]{:S(2)}) %collective-permute-start.8) | collective-permute-done | bytes 81952 | tf_op jit(solution)/shard_map/ppermute | solution.py:183
  37.3 1.6 %collective-permute-done.9 = f32[80,256]{1,0:T(8,128)S(1)} collective-permute-done((f32[80,256]{1,0:T(8,128)S(1)}, f32[80,256]{1,0:T(8,128)S(1)}, u32[]{:S(2)}, u32[]{:S(2)}) %collective-permute-start.9) | collective-permute-done | bytes 81952 | tf_op jit(solution)/shard_map/ppermute | solution.py:183
  40.4 2.1 %collective-permute-start.12 = (f32[64,256]{1,0:T(8,128)S(1)}, f32[64,256]{1,0:T(8,128)S(1)}, u32[]{:S(2)}, u32[]{:S(2)}) collective-permute-start(f32[64,256]{1,0:T(8,128)S(1)} %fusion.9), channel_id=1, source_target_pairs={{0,3},{1,2},{2,1},{3,0},{4,7},{5,6},{6,5},{7,4},{8,11},{9,10},{10,... | collective-permute-start | bytes 196616 | tf_op jit(solution)/shard_map/ppermute | solution.py:183
  42.5 1.6 %collective-permute-start.13 = (f32[144,256]{1,0:T(8,128)S(1)}, f32[144,256]{1,0:T(8,128)S(1)}, u32[]{:S(2)}, u32[]{:S(2)}) collective-permute-start(f32[144,256]{1,0:T(8,128)S(1)} %pad_maximum_fusion.15), channel_id=1, source_target_pairs={{0,8},{4,12},{8,0},{12,4},{16,24},{20,28},{24,16},{28,20},{1,9},{5... | collective-permute-start | bytes 442376 | tf_op jit(solution)/shard_map/ppermute | solution.py:183
  44.2 1.4 %collective-permute-done.12 = f32[64,256]{1,0:T(8,128)S(1)} collective-permute-done((f32[64,256]{1,0:T(8,128)S(1)}, f32[64,256]{1,0:T(8,128)S(1)}, u32[]{:S(2)}, u32[]{:S(2)}) %collective-permute-start.12) | collective-permute-done | bytes 65568 | tf_op jit(solution)/shard_map/ppermute | solution.py:183
  45.7 2.0 %collective-permute-done.13 = f32[144,256]{1,0:T(8,128)S(1)} collective-permute-done((f32[144,256]{1,0:T(8,128)S(1)}, f32[144,256]{1,0:T(8,128)S(1)}, u32[]{:S(2)}, u32[]{:S(2)}) %collective-permute-start.13) | collective-permute-done | bytes 147488 | tf_op jit(solution)/shard_map/ppermute | solution.py:183
  47.7 3.8 %collective-permute-start.14 = (f32[144,256]{1,0:T(8,128)S(1)}, f32[144,256]{1,0:T(8,128)S(1)}, u32[]{:S(2)}, u32[]{:S(2)}) collective-permute-start(f32[144,256]{1,0:T(8,128)S(1)} %fusion.17), channel_id=1, source_target_pairs={{0,24},{4,28},{8,16},{12,20},{16,8},{20,12},{24,0},{28,4},{1,25},{... | collective-permute-start | bytes 442376 | tf_op jit(solution)/shard_map/ppermute | solution.py:183
  51.5 3.3 %collective-permute-done.14 = f32[144,256]{1,0:T(8,128)S(1)} collective-permute-done((f32[144,256]{1,0:T(8,128)S(1)}, f32[144,256]{1,0:T(8,128)S(1)}, u32[]{:S(2)}, u32[]{:S(2)}) %collective-permute-start.14) | collective-permute-done | bytes 147488 | tf_op jit(solution)/shard_map/ppermute | solution.py:183
  56.4 12.2 %shard_map.70 = (f32[256,256]{1,0:T(8,128)S(1)}, f32[144,256]{1,0:T(8,128)S(1)}, f32[144,256]{1,0:T(8,128)S(1)}) custom-call(s32[256,32,256]{2,1,0:T(8,128)} %obs_hbm.5, s32[2,256,8,128]{3,2,1,0:T(8,128)S(1)} %shard_map.68.head_ref, f32[256,256]{1,0:T(8,128)S(1)} %fusion.a_ref, f32[256,256]{1,0:T(8,128)S(1)} %bitcast.120, ...), custom_call_target="tpu_custom_call" | custom-call | flops 9663676416 | bytes 8388608 | tf_op jit(solution)/shard_map/pallas_call | solution.py:133
  71.6 2.1 %collective-permute-start.19 = (f32[80,256]{1,0:T(8,128)S(1)}, f32[80,256]{1,0:T(8,128)S(1)}, u32[]{:S(2)}, u32[]{:S(2)}) collective-permute-start(f32[80,256]{1,0:T(8,128)S(1)} %get-tuple-element.60), channel_id=1, source_target_pairs={{0,3},{1,2},{2,1},{3,0},{4,7},{5,6},{6,5},{7,4},{8,11},{9,10},{10,... | collective-permute-start | bytes 245768 | tf_op jit(solution)/shard_map/ppermute | solution.py:183
  77.0 1.6 %collective-permute-start.20 = (f32[48,256]{1,0:T(8,128)S(1)}, f32[48,256]{1,0:T(8,128)S(1)}, u32[]{:S(2)}, u32[]{:S(2)}) collective-permute-start(f32[48,256]{1,0:T(8,128)S(1)} %get-tuple-element.58), channel_id=1, source_target_pairs={{0,8},{4,12},{8,0},{12,4},{16,24},{20,28},{24,16},{28,20},{1,9},{5... | collective-permute-start | bytes 147464 | tf_op jit(solution)/shard_map/ppermute | solution.py:183
  78.7 2.6 %collective-permute-start.21 = (f32[48,256]{1,0:T(8,128)S(1)}, f32[48,256]{1,0:T(8,128)S(1)}, u32[]{:S(2)}, u32[]{:S(2)}) collective-permute-start(f32[48,256]{1,0:T(8,128)S(1)} %get-tuple-element.59), channel_id=1, source_target_pairs={{0,16},{4,20},{8,24},{12,28},{16,0},{20,4},{24,8},{28,12},{1,17},{... | collective-permute-start | bytes 147464 | tf_op jit(solution)/shard_map/ppermute | solution.py:183
  82.2 3.0 %collective-permute-done.21 = f32[48,256]{1,0:T(8,128)S(1)} collective-permute-done((f32[48,256]{1,0:T(8,128)S(1)}, f32[48,256]{1,0:T(8,128)S(1)}, u32[]{:S(2)}, u32[]{:S(2)}) %collective-permute-start.21) | collective-permute-done | bytes 49184 | tf_op jit(solution)/shard_map/ppermute | solution.py:183
  85.2 1.9 %collective-permute-done.22 = f32[48,256]{1,0:T(8,128)S(1)} collective-permute-done((f32[48,256]{1,0:T(8,128)S(1)}, f32[48,256]{1,0:T(8,128)S(1)}, u32[]{:S(2)}, u32[]{:S(2)}) %collective-permute-start.22) | collective-permute-done | bytes 49184 | tf_op jit(solution)/shard_map/ppermute | solution.py:183
  (92 shorter events, 16.6 us)
Async XLA Ops:
  0.6 11.8 %collective-permute-start = (f32[64,256]{1,0:T(8,128)}, f32[64,256]{1,0:T(8,128)S(1)}, u32[]{:S(2)}, u32[]{:S(2)}) collective-permute-start(f32[64,256]{1,0:T(8,128)} %a_hbm.1), channel_id=1, source_target_pairs={{0,1},{1,0},{2,3},{3,2},{4,5},{5,4},{6,7},{7,6},{8,9},{9,8},{10,11... | collective-permute-start | bytes 196616 | tf_op jit(solution)/shard_map/ppermute | solution.py:183
  3.7 8.8 %collective-permute-start.1 = (f32[64,256]{1,0:T(8,128)}, f32[64,256]{1,0:T(8,128)S(1)}, u32[]{:S(2)}, u32[]{:S(2)}) collective-permute-start(f32[64,256]{1,0:T(8,128)} %a_hbm.1), channel_id=1, source_target_pairs={{0,2},{1,3},{2,0},{3,1},{4,6},{5,7},{6,4},{7,5},{8,10},{9,11},{10,... | collective-permute-start | bytes 196616 | tf_op jit(solution)/shard_map/ppermute | solution.py:183
  5.2 7.2 %collective-permute-start.2 = (f32[64,256]{1,0:T(8,128)}, f32[64,256]{1,0:T(8,128)S(1)}, u32[]{:S(2)}, u32[]{:S(2)}) collective-permute-start(f32[64,256]{1,0:T(8,128)} %a_hbm.1), channel_id=1, source_target_pairs={{0,3},{1,2},{2,1},{3,0},{4,7},{5,6},{6,5},{7,4},{8,11},{9,10},{10,... | collective-permute-start | bytes 196616 | tf_op jit(solution)/shard_map/ppermute | solution.py:183
  5.2 5.6 %collective-permute-start.3 = (f32[1,32,256]{2,1,0:T(8,128)}, f32[1,32,256]{2,1,0:T(8,128)S(1)}, u32[]{:S(2)}, u32[]{:S(2)}) collective-permute-start(f32[1,32,256]{2,1,0:T(8,128)} %bitcast.148), channel_id=1, source_target_pairs={{0,16},{4,20},{8,24},{12,28},{16,0},{20,4},{24,8},{28,12},{1,17},{... | collective-permute-start | bytes 98312 | tf_op jit(solution)/shard_map/ppermute | solution.py:183
  10.8 4.3 %collective-permute-start.4 = (f32[2,32,256]{2,1,0:T(8,128)S(1)}, f32[2,32,256]{2,1,0:T(8,128)S(1)}, u32[]{:S(2)}, u32[]{:S(2)}) collective-permute-start(f32[2,32,256]{2,1,0:T(8,128)S(1)} %pad_maximum_fusion.24), channel_id=1, source_target_pairs={{0,8},{4,12},{8,0},{12,4},{16,24},{20,28},{24,16},{28,20},{1,9},{5... | collective-permute-start | bytes 196616 | tf_op jit(solution)/shard_map/ppermute | solution.py:183
  15.3 1.4 %collective-permute-start.5 = (f32[144,256]{1,0:T(8,128)S(1)}, f32[144,256]{1,0:T(8,128)S(1)}, u32[]{:S(2)}, u32[]{:S(2)}) collective-permute-start(f32[144,256]{1,0:T(8,128)S(1)} %pad_maximum_fusion.14), channel_id=1, source_target_pairs={{0,4},{4,0},{8,12},{12,8},{16,20},{20,16},{24,28},{28,24},{1,5},{5... | collective-permute-start | bytes 442376 | tf_op jit(solution)/shard_map/ppermute | solution.py:183
  29.0 1.4 %collective-permute-start.6 = (f32[144,256]{1,0:T(8,128)S(1)}, f32[144,256]{1,0:T(8,128)S(1)}, u32[]{:S(2)}, u32[]{:S(2)}) collective-permute-start(f32[144,256]{1,0:T(8,128)S(1)} %get-tuple-element.17), channel_id=1, source_target_pairs={{0,4},{4,0},{8,12},{12,8},{16,20},{20,16},{24,28},{28,24},{1,5},{5... | collective-permute-start | bytes 442376 | tf_op jit(solution)/shard_map/ppermute | solution.py:183
  30.5 4.6 %collective-permute-start.7 = (f32[80,256]{1,0:T(8,128)S(1)}, f32[80,256]{1,0:T(8,128)S(1)}, u32[]{:S(2)}, u32[]{:S(2)}) collective-permute-start(f32[80,256]{1,0:T(8,128)S(1)} %get-tuple-element.64), channel_id=1, source_target_pairs={{0,1},{1,0},{2,3},{3,2},{4,5},{5,4},{6,7},{7,6},{8,9},{9,8},{10,11... | collective-permute-start | bytes 245768 | tf_op jit(solution)/shard_map/ppermute | solution.py:183
  32.0 5.3 %collective-permute-start.8 = (f32[80,256]{1,0:T(8,128)S(1)}, f32[80,256]{1,0:T(8,128)S(1)}, u32[]{:S(2)}, u32[]{:S(2)}) collective-permute-start(f32[80,256]{1,0:T(8,128)S(1)} %get-tuple-element.65), channel_id=1, source_target_pairs={{0,2},{1,3},{2,0},{3,1},{4,6},{5,7},{6,4},{7,5},{8,10},{9,11},{10,... | collective-permute-start | bytes 245768 | tf_op jit(solution)/shard_map/ppermute | solution.py:183
  33.5 5.3 %collective-permute-start.9 = (f32[80,256]{1,0:T(8,128)S(1)}, f32[80,256]{1,0:T(8,128)S(1)}, u32[]{:S(2)}, u32[]{:S(2)}) collective-permute-start(f32[80,256]{1,0:T(8,128)S(1)} %get-tuple-element.63), channel_id=1, source_target_pairs={{0,3},{1,2},{2,1},{3,0},{4,7},{5,6},{6,5},{7,4},{8,11},{9,10},{10,... | collective-permute-start | bytes 245768 | tf_op jit(solution)/shard_map/ppermute | solution.py:183
  38.9 5.2 %collective-permute-start.10 = (f32[64,256]{1,0:T(8,128)S(1)}, f32[64,256]{1,0:T(8,128)S(1)}, u32[]{:S(2)}, u32[]{:S(2)}) collective-permute-start(f32[64,256]{1,0:T(8,128)S(1)} %fusion.9), channel_id=1, source_target_pairs={{0,1},{1,0},{2,3},{3,2},{4,5},{5,4},{6,7},{7,6},{8,9},{9,8},{10,11... | collective-permute-start | bytes 196616 | tf_op jit(solution)/shard_map/ppermute | solution.py:183
  39.5 4.6 %collective-permute-start.11 = (f32[64,256]{1,0:T(8,128)S(1)}, f32[64,256]{1,0:T(8,128)S(1)}, u32[]{:S(2)}, u32[]{:S(2)}) collective-permute-start(f32[64,256]{1,0:T(8,128)S(1)} %fusion.9), channel_id=1, source_target_pairs={{0,2},{1,3},{2,0},{3,1},{4,6},{5,7},{6,4},{7,5},{8,10},{9,11},{10,... | collective-permute-start | bytes 196616 | tf_op jit(solution)/shard_map/ppermute | solution.py:183
  40.4 5.2 %collective-permute-start.12 = (f32[64,256]{1,0:T(8,128)S(1)}, f32[64,256]{1,0:T(8,128)S(1)}, u32[]{:S(2)}, u32[]{:S(2)}) collective-permute-start(f32[64,256]{1,0:T(8,128)S(1)} %fusion.9), channel_id=1, source_target_pairs={{0,3},{1,2},{2,1},{3,0},{4,7},{5,6},{6,5},{7,4},{8,11},{9,10},{10,... | collective-permute-start | bytes 196616 | tf_op jit(solution)/shard_map/ppermute | solution.py:183
  42.5 5.2 %collective-permute-start.13 = (f32[144,256]{1,0:T(8,128)S(1)}, f32[144,256]{1,0:T(8,128)S(1)}, u32[]{:S(2)}, u32[]{:S(2)}) collective-permute-start(f32[144,256]{1,0:T(8,128)S(1)} %pad_maximum_fusion.15), channel_id=1, source_target_pairs={{0,8},{4,12},{8,0},{12,4},{16,24},{20,28},{24,16},{28,20},{1,9},{5... | collective-permute-start | bytes 442376 | tf_op jit(solution)/shard_map/ppermute | solution.py:183
  47.7 7.1 %collective-permute-start.14 = (f32[144,256]{1,0:T(8,128)S(1)}, f32[144,256]{1,0:T(8,128)S(1)}, u32[]{:S(2)}, u32[]{:S(2)}) collective-permute-start(f32[144,256]{1,0:T(8,128)S(1)} %fusion.17), channel_id=1, source_target_pairs={{0,24},{4,28},{8,16},{12,20},{16,8},{20,12},{24,0},{28,4},{1,25},{... | collective-permute-start | bytes 442376 | tf_op jit(solution)/shard_map/ppermute | solution.py:183
  54.9 1.4 %collective-permute-start.15 = (f32[144,256]{1,0:T(8,128)S(1)}, f32[144,256]{1,0:T(8,128)S(1)}, u32[]{:S(2)}, u32[]{:S(2)}) collective-permute-start(f32[144,256]{1,0:T(8,128)S(1)} %pad_maximum_fusion.16), channel_id=1, source_target_pairs={{0,4},{4,0},{8,12},{12,8},{16,20},{20,16},{24,28},{28,24},{1,5},{5... | collective-permute-start | bytes 442376 | tf_op jit(solution)/shard_map/ppermute | solution.py:183
  68.7 1.4 %collective-permute-start.16 = (f32[144,256]{1,0:T(8,128)S(1)}, f32[144,256]{1,0:T(8,128)S(1)}, u32[]{:S(2)}, u32[]{:S(2)}) collective-permute-start(f32[144,256]{1,0:T(8,128)S(1)} %get-tuple-element.20), channel_id=1, source_target_pairs={{0,4},{4,0},{8,12},{12,8},{16,20},{20,16},{24,28},{28,24},{1,5},{5... | collective-permute-start | bytes 442376 | tf_op jit(solution)/shard_map/ppermute | solution.py:183
  70.2 4.9 %collective-permute-start.17 = (f32[80,256]{1,0:T(8,128)S(1)}, f32[80,256]{1,0:T(8,128)S(1)}, u32[]{:S(2)}, u32[]{:S(2)}) collective-permute-start(f32[80,256]{1,0:T(8,128)S(1)} %get-tuple-element.61), channel_id=1, source_target_pairs={{0,1},{1,0},{2,3},{3,2},{4,5},{5,4},{6,7},{7,6},{8,9},{9,8},{10,11... | collective-permute-start | bytes 245768 | tf_op jit(solution)/shard_map/ppermute | solution.py:183
  70.8 5.3 %collective-permute-start.18 = (f32[80,256]{1,0:T(8,128)S(1)}, f32[80,256]{1,0:T(8,128)S(1)}, u32[]{:S(2)}, u32[]{:S(2)}) collective-permute-start(f32[80,256]{1,0:T(8,128)S(1)} %get-tuple-element.62), channel_id=1, source_target_pairs={{0,2},{1,3},{2,0},{3,1},{4,6},{5,7},{6,4},{7,5},{8,10},{9,11},{10,... | collective-permute-start | bytes 245768 | tf_op jit(solution)/shard_map/ppermute | solution.py:183
  71.6 5.3 %collective-permute-start.19 = (f32[80,256]{1,0:T(8,128)S(1)}, f32[80,256]{1,0:T(8,128)S(1)}, u32[]{:S(2)}, u32[]{:S(2)}) collective-permute-start(f32[80,256]{1,0:T(8,128)S(1)} %get-tuple-element.60), channel_id=1, source_target_pairs={{0,3},{1,2},{2,1},{3,0},{4,7},{5,6},{6,5},{7,4},{8,11},{9,10},{10,... | collective-permute-start | bytes 245768 | tf_op jit(solution)/shard_map/ppermute | solution.py:183
  77.0 5.2 %collective-permute-start.20 = (f32[48,256]{1,0:T(8,128)S(1)}, f32[48,256]{1,0:T(8,128)S(1)}, u32[]{:S(2)}, u32[]{:S(2)}) collective-permute-start(f32[48,256]{1,0:T(8,128)S(1)} %get-tuple-element.58), channel_id=1, source_target_pairs={{0,8},{4,12},{8,0},{12,4},{16,24},{20,28},{24,16},{28,20},{1,9},{5... | collective-permute-start | bytes 147464 | tf_op jit(solution)/shard_map/ppermute | solution.py:183
  78.7 6.6 %collective-permute-start.21 = (f32[48,256]{1,0:T(8,128)S(1)}, f32[48,256]{1,0:T(8,128)S(1)}, u32[]{:S(2)}, u32[]{:S(2)}) collective-permute-start(f32[48,256]{1,0:T(8,128)S(1)} %get-tuple-element.59), channel_id=1, source_target_pairs={{0,16},{4,20},{8,24},{12,28},{16,0},{20,4},{24,8},{28,12},{1,17},{... | collective-permute-start | bytes 147464 | tf_op jit(solution)/shard_map/ppermute | solution.py:183
  81.3 5.9 %collective-permute-start.22 = (f32[48,256]{1,0:T(8,128)S(1)}, f32[48,256]{1,0:T(8,128)S(1)}, u32[]{:S(2)}, u32[]{:S(2)}) collective-permute-start(f32[48,256]{1,0:T(8,128)S(1)} %get-tuple-element.57), channel_id=1, source_target_pairs={{0,24},{4,28},{8,16},{12,20},{16,8},{20,12},{24,0},{28,4},{1,25},{... | collective-permute-start | bytes 147464 | tf_op jit(solution)/shard_map/ppermute | solution.py:183
  87.2 1.2 %collective-permute-start.23 = (f32[16,256]{1,0:T(8,128)S(1)}, f32[16,256]{1,0:T(8,128)S(1)}, u32[]{:S(2)}, u32[]{:S(2)}) collective-permute-start(f32[16,256]{1,0:T(8,128)S(1)} %fusion.14), channel_id=1, source_target_pairs={{0,4},{4,0},{8,12},{12,8},{16,20},{20,16},{24,28},{28,24},{1,5},{5... | collective-permute-start | bytes 49160 | tf_op jit(solution)/shard_map/ppermute | solution.py:183
  (2 other events, 31.9 us)

commit v3 on v2

--- a/solution.py
+++ b/solution.py
@@ -41,7 +41,7 @@
     b = b_ref[...]
     bh, bl = split(b)
     b_cat[...] = jnp.concatenate([bh, bl, bh], 0)
-    bth, btl = split(b.T)
+    bth, btl = split(0.5 * b.T)
     bt_cat[...] = jnp.concatenate([bth, btl, bth], 0)
     ath, atl = split(a_ref[...].T)
     at_cat[...] = jnp.concatenate([ath, ath, atl], 1)
@@ -75,7 +75,7 @@
             x = jnp.concatenate([
                 jnp.concatenate([p[pl.ds(k, n, stride=depth_block), :] for p in flat], 1)
                 for k in range(k0, k0 + group)], 0)
-            derivative = 0.5 * jnp.tanh(0.5 * logits) + (0.5 - x.astype(f32))
+            derivative = 0.5 * jnp.tanh(logits) + (0.5 - x.astype(f32))
             dh, dw = split(derivative)
             carried = jnp.dot(
                 jnp.concatenate([dh, dh, dw], 1), b_cat[...], preferred_element_type=f32)
@@ -128,7 +128,7 @@
     rank = a.shape[1]
     panels, _, depth_block, lanes = head.shape
     blocks = depth // depth_block
-    group = 1
+    group = 2
     here = pl.BlockSpec(memory_space=pltpu.VMEM)
     return pl.pallas_call(
         functools.partial(grad_kernel, group=group, cols_own=cols_own),

time: 89.2 us -> 88.4 us (level)
  no operation moved by 1% of the time
where the time goes in v3:
time: 88.4 us; the launch traced here: 88.2 us
  starting transfers between devices  30.5 us (35%)
  waiting for transfers between devices  27.8 us (31%)
  Pallas kernels  26 us (29%)
  other arithmetic  2.6 us (3%)
  between operations  1.11 us (1%)
    ppermute x24, starting transfers between devices, exchange(): return lax.ppermute(x, axis, [(i, i ^ mask) for i in range(n)])  30.5 us
    ppermute x24, waiting for transfers between devices, exchange(): return lax.ppermute(x, axis, [(i, i ^ mask) for i in range(n)])  27.8 us
    pallas_call x2, Pallas kernels, gradients(): pl.pallas_call(functools.partial(grad_kernel, group=group, cols_own=cols_...  23.5 us
  transfers between devices with their start and end apart: 24, of which 17 were waited for; matrix products, arithmetic and copies ran while one was open for 2% of the time, Pallas kernels for 3%

profile of v3, /device:TPU:0, one launch (start us, length us, event | category | flops | bytes accessed | tf_op | source)
XLA Modules:
  0.0 88.2 jit_solution(16182002005985691401)
XLA Ops:
  0.6 3.0 %collective-permute-start = (f32[64,256]{1,0:T(8,128)}, f32[64,256]{1,0:T(8,128)S(1)}, u32[]{:S(2)}, u32[]{:S(2)}) collective-permute-start(f32[64,256]{1,0:T(8,128)} %a_hbm.1), channel_id=1, source_target_pairs={{0,1},{1,0},{2,3},{3,2},{4,5},{5,4},{6,7},{7,6},{8,9},{9,8},{10,11... | collective-permute-start | bytes 196616 | tf_op jit(solution)/shard_map/ppermute | solution.py:183
  3.7 1.5 %collective-permute-start.1 = (f32[64,256]{1,0:T(8,128)}, f32[64,256]{1,0:T(8,128)S(1)}, u32[]{:S(2)}, u32[]{:S(2)}) collective-permute-start(f32[64,256]{1,0:T(8,128)} %a_hbm.1), channel_id=1, source_target_pairs={{0,2},{1,3},{2,0},{3,1},{4,6},{5,7},{6,4},{7,5},{8,10},{9,11},{10,... | collective-permute-start | bytes 196616 | tf_op jit(solution)/shard_map/ppermute | solution.py:183
  5.2 3.0 %collective-permute-start.3 = (f32[1,32,256]{2,1,0:T(8,128)}, f32[1,32,256]{2,1,0:T(8,128)S(1)}, u32[]{:S(2)}, u32[]{:S(2)}) collective-permute-start(f32[1,32,256]{2,1,0:T(8,128)} %bitcast.148), channel_id=1, source_target_pairs={{0,16},{4,20},{8,24},{12,28},{16,0},{20,4},{24,8},{28,12},{1,17},{... | collective-permute-start | bytes 98312 | tf_op jit(solution)/shard_map/ppermute | solution.py:183
  9.2 1.6 %shard_map.68.head_ref = s32[2,256,8,128]{3,2,1,0:T(8,128)S(1)} custom-call(s32[256,32,256]{2,1,0:T(8,128)} %obs_hbm.5), custom_call_target="tpu_custom_call" | custom-call | tf_op jit(solution)/shard_map/pallas_call | solution.py:171
  10.8 1.6 %collective-permute-start.4 = (f32[2,32,256]{2,1,0:T(8,128)S(1)}, f32[2,32,256]{2,1,0:T(8,128)S(1)}, u32[]{:S(2)}, u32[]{:S(2)}) collective-permute-start(f32[2,32,256]{2,1,0:T(8,128)S(1)} %pad_maximum_fusion.24), channel_id=1, source_target_pairs={{0,8},{4,12},{8,0},{12,4},{16,24},{20,28},{24,16},{28,20},{1,9},{5... | collective-permute-start | bytes 196616 | tf_op jit(solution)/shard_map/ppermute | solution.py:183
  12.6 2.5 %collective-permute-done.4 = f32[2,32,256]{2,1,0:T(8,128)S(1)} collective-permute-done((f32[2,32,256]{2,1,0:T(8,128)S(1)}, f32[2,32,256]{2,1,0:T(8,128)S(1)}, u32[]{:S(2)}, u32[]{:S(2)}) %collective-permute-start.4) | collective-permute-done | bytes 65568 | tf_op jit(solution)/shard_map/ppermute | solution.py:183
  15.4 1.3 %collective-permute-done.5 = f32[144,256]{1,0:T(8,128)S(1)} collective-permute-done((f32[144,256]{1,0:T(8,128)S(1)}, f32[144,256]{1,0:T(8,128)S(1)}, u32[]{:S(2)}, u32[]{:S(2)}) %collective-permute-start.5) | collective-permute-done | bytes 147488 | tf_op jit(solution)/shard_map/ppermute | solution.py:183
  16.8 11.7 %shard_map.69 = (f32[256,256]{1,0:T(8,128)S(1)}, f32[144,256]{1,0:T(8,128)S(1)}, f32[144,256]{1,0:T(8,128)S(1)}) custom-call(s32[256,32,256]{2,1,0:T(8,128)} %obs_hbm.5, s32[2,256,8,128]{3,2,1,0:T(8,128)S(1)} %shard_map.68.head_ref, f32[256,256]{1,0:T(8,128)S(1)} %fusion.1.a_ref, f32[256,256]{1,0:T(8,128)S(1)} %bitcast.121, ...), custom_call_target="tpu_custom_call" | custom-call | flops 9663676416 | bytes 8388608 | tf_op jit(solution)/shard_map/pallas_call | solution.py:133
  30.0 1.6 %collective-permute-start.7 = (f32[80,256]{1,0:T(8,128)S(1)}, f32[80,256]{1,0:T(8,128)S(1)}, u32[]{:S(2)}, u32[]{:S(2)}) collective-permute-start(f32[80,256]{1,0:T(8,128)S(1)} %get-tuple-element.64), channel_id=1, source_target_pairs={{0,1},{1,0},{2,3},{3,2},{4,5},{5,4},{6,7},{7,6},{8,9},{9,8},{10,11... | collective-permute-start | bytes 245768 | tf_op jit(solution)/shard_map/ppermute | solution.py:183
  31.6 1.5 %collective-permute-start.8 = (f32[80,256]{1,0:T(8,128)S(1)}, f32[80,256]{1,0:T(8,128)S(1)}, u32[]{:S(2)}, u32[]{:S(2)}) collective-permute-start(f32[80,256]{1,0:T(8,128)S(1)} %get-tuple-element.65), channel_id=1, source_target_pairs={{0,2},{1,3},{2,0},{3,1},{4,6},{5,7},{6,4},{7,5},{8,10},{9,11},{10,... | collective-permute-start | bytes 245768 | tf_op jit(solution)/shard_map/ppermute | solution.py:183
  34.6 2.3 %collective-permute-done.8 = f32[80,256]{1,0:T(8,128)S(1)} collective-permute-done((f32[80,256]{1,0:T(8,128)S(1)}, f32[80,256]{1,0:T(8,128)S(1)}, u32[]{:S(2)}, u32[]{:S(2)}) %collective-permute-start.8) | collective-permute-done | bytes 81952 | tf_op jit(solution)/shard_map/ppermute | solution.py:183
  36.8 1.6 %collective-permute-done.9 = f32[80,256]{1,0:T(8,128)S(1)} collective-permute-done((f32[80,256]{1,0:T(8,128)S(1)}, f32[80,256]{1,0:T(8,128)S(1)}, u32[]{:S(2)}, u32[]{:S(2)}) %collective-permute-start.9) | collective-permute-done | bytes 81952 | tf_op jit(solution)/shard_map/ppermute | solution.py:183
  40.0 2.1 %collective-permute-start.12 = (f32[64,256]{1,0:T(8,128)S(1)}, f32[64,256]{1,0:T(8,128)S(1)}, u32[]{:S(2)}, u32[]{:S(2)}) collective-permute-start(f32[64,256]{1,0:T(8,128)S(1)} %fusion.9), channel_id=1, source_target_pairs={{0,3},{1,2},{2,1},{3,0},{4,7},{5,6},{6,5},{7,4},{8,11},{9,10},{10,... | collective-permute-start | bytes 196616 | tf_op jit(solution)/shard_map/ppermute | solution.py:183
  42.1 1.6 %collective-permute-start.13 = (f32[144,256]{1,0:T(8,128)S(1)}, f32[144,256]{1,0:T(8,128)S(1)}, u32[]{:S(2)}, u32[]{:S(2)}) collective-permute-start(f32[144,256]{1,0:T(8,128)S(1)} %pad_maximum_fusion.15), channel_id=1, source_target_pairs={{0,8},{4,12},{8,0},{12,4},{16,24},{20,28},{24,16},{28,20},{1,9},{5... | collective-permute-start | bytes 442376 | tf_op jit(solution)/shard_map/ppermute | solution.py:183
  43.7 1.4 %collective-permute-done.12 = f32[64,256]{1,0:T(8,128)S(1)} collective-permute-done((f32[64,256]{1,0:T(8,128)S(1)}, f32[64,256]{1,0:T(8,128)S(1)}, u32[]{:S(2)}, u32[]{:S(2)}) %collective-permute-start.12) | collective-permute-done | bytes 65568 | tf_op jit(solution)/shard_map/ppermute | solution.py:183
  45.2 2.0 %collective-permute-done.13 = f32[144,256]{1,0:T(8,128)S(1)} collective-permute-done((f32[144,256]{1,0:T(8,128)S(1)}, f32[144,256]{1,0:T(8,128)S(1)}, u32[]{:S(2)}, u32[]{:S(2)}) %collective-permute-start.13) | collective-permute-done | bytes 147488 | tf_op jit(solution)/shard_map/ppermute | solution.py:183
  47.3 3.8 %collective-permute-start.14 = (f32[144,256]{1,0:T(8,128)S(1)}, f32[144,256]{1,0:T(8,128)S(1)}, u32[]{:S(2)}, u32[]{:S(2)}) collective-permute-start(f32[144,256]{1,0:T(8,128)S(1)} %fusion.17), channel_id=1, source_target_pairs={{0,24},{4,28},{8,16},{12,20},{16,8},{20,12},{24,0},{28,4},{1,25},{... | collective-permute-start | bytes 442376 | tf_op jit(solution)/shard_map/ppermute | solution.py:183
  51.1 3.3 %collective-permute-done.14 = f32[144,256]{1,0:T(8,128)S(1)} collective-permute-done((f32[144,256]{1,0:T(8,128)S(1)}, f32[144,256]{1,0:T(8,128)S(1)}, u32[]{:S(2)}, u32[]{:S(2)}) %collective-permute-start.14) | collective-permute-done | bytes 147488 | tf_op jit(solution)/shard_map/ppermute | solution.py:183
  56.0 11.8 %shard_map.70 = (f32[256,256]{1,0:T(8,128)S(1)}, f32[144,256]{1,0:T(8,128)S(1)}, f32[144,256]{1,0:T(8,128)S(1)}) custom-call(s32[256,32,256]{2,1,0:T(8,128)} %obs_hbm.5, s32[2,256,8,128]{3,2,1,0:T(8,128)S(1)} %shard_map.68.head_ref, f32[256,256]{1,0:T(8,128)S(1)} %fusion.a_ref, f32[256,256]{1,0:T(8,128)S(1)} %bitcast.120, ...), custom_call_target="tpu_custom_call" | custom-call | flops 9663676416 | bytes 8388608 | tf_op jit(solution)/shard_map/pallas_call | solution.py:133
  70.8 2.1 %collective-permute-start.19 = (f32[80,256]{1,0:T(8,128)S(1)}, f32[80,256]{1,0:T(8,128)S(1)}, u32[]{:S(2)}, u32[]{:S(2)}) collective-permute-start(f32[80,256]{1,0:T(8,128)S(1)} %get-tuple-element.60), channel_id=1, source_target_pairs={{0,3},{1,2},{2,1},{3,0},{4,7},{5,6},{6,5},{7,4},{8,11},{9,10},{10,... | collective-permute-start | bytes 245768 | tf_op jit(solution)/shard_map/ppermute | solution.py:183
  76.2 1.6 %collective-permute-start.20 = (f32[48,256]{1,0:T(8,128)S(1)}, f32[48,256]{1,0:T(8,128)S(1)}, u32[]{:S(2)}, u32[]{:S(2)}) collective-permute-start(f32[48,256]{1,0:T(8,128)S(1)} %get-tuple-element.58), channel_id=1, source_target_pairs={{0,8},{4,12},{8,0},{12,4},{16,24},{20,28},{24,16},{28,20},{1,9},{5... | collective-permute-start | bytes 147464 | tf_op jit(solution)/shard_map/ppermute | solution.py:183
  77.8 2.6 %collective-permute-start.21 = (f32[48,256]{1,0:T(8,128)S(1)}, f32[48,256]{1,0:T(8,128)S(1)}, u32[]{:S(2)}, u32[]{:S(2)}) collective-permute-start(f32[48,256]{1,0:T(8,128)S(1)} %get-tuple-element.59), channel_id=1, source_target_pairs={{0,16},{4,20},{8,24},{12,28},{16,0},{20,4},{24,8},{28,12},{1,17},{... | collective-permute-start | bytes 147464 | tf_op jit(solution)/shard_map/ppermute | solution.py:183
  81.4 3.0 %collective-permute-done.21 = f32[48,256]{1,0:T(8,128)S(1)} collective-permute-done((f32[48,256]{1,0:T(8,128)S(1)}, f32[48,256]{1,0:T(8,128)S(1)}, u32[]{:S(2)}, u32[]{:S(2)}) %collective-permute-start.21) | collective-permute-done | bytes 49184 | tf_op jit(solution)/shard_map/ppermute | solution.py:183
  84.4 1.9 %collective-permute-done.22 = f32[48,256]{1,0:T(8,128)S(1)} collective-permute-done((f32[48,256]{1,0:T(8,128)S(1)}, f32[48,256]{1,0:T(8,128)S(1)}, u32[]{:S(2)}, u32[]{:S(2)}) %collective-permute-start.22) | collective-permute-done | bytes 49184 | tf_op jit(solution)/shard_map/ppermute | solution.py:183
  (92 shorter events, 16.5 us)
Async XLA Ops:
  0.6 11.8 %collective-permute-start = (f32[64,256]{1,0:T(8,128)}, f32[64,256]{1,0:T(8,128)S(1)}, u32[]{:S(2)}, u32[]{:S(2)}) collective-permute-start(f32[64,256]{1,0:T(8,128)} %a_hbm.1), channel_id=1, source_target_pairs={{0,1},{1,0},{2,3},{3,2},{4,5},{5,4},{6,7},{7,6},{8,9},{9,8},{10,11... | collective-permute-start | bytes 196616 | tf_op jit(solution)/shard_map/ppermute | solution.py:183
  3.7 8.8 %collective-permute-start.1 = (f32[64,256]{1,0:T(8,128)}, f32[64,256]{1,0:T(8,128)S(1)}, u32[]{:S(2)}, u32[]{:S(2)}) collective-permute-start(f32[64,256]{1,0:T(8,128)} %a_hbm.1), channel_id=1, source_target_pairs={{0,2},{1,3},{2,0},{3,1},{4,6},{5,7},{6,4},{7,5},{8,10},{9,11},{10,... | collective-permute-start | bytes 196616 | tf_op jit(solution)/shard_map/ppermute | solution.py:183
  5.2 7.2 %collective-permute-start.2 = (f32[64,256]{1,0:T(8,128)}, f32[64,256]{1,0:T(8,128)S(1)}, u32[]{:S(2)}, u32[]{:S(2)}) collective-permute-start(f32[64,256]{1,0:T(8,128)} %a_hbm.1), channel_id=1, source_target_pairs={{0,3},{1,2},{2,1},{3,0},{4,7},{5,6},{6,5},{7,4},{8,11},{9,10},{10,... | collective-permute-start | bytes 196616 | tf_op jit(solution)/shard_map/ppermute | solution.py:183
  5.2 5.6 %collective-permute-start.3 = (f32[1,32,256]{2,1,0:T(8,128)}, f32[1,32,256]{2,1,0:T(8,128)S(1)}, u32[]{:S(2)}, u32[]{:S(2)}) collective-permute-start(f32[1,32,256]{2,1,0:T(8,128)} %bitcast.148), channel_id=1, source_target_pairs={{0,16},{4,20},{8,24},{12,28},{16,0},{20,4},{24,8},{28,12},{1,17},{... | collective-permute-start | bytes 98312 | tf_op jit(solution)/shard_map/ppermute | solution.py:183
  10.8 4.3 %collective-permute-start.4 = (f32[2,32,256]{2,1,0:T(8,128)S(1)}, f32[2,32,256]{2,1,0:T(8,128)S(1)}, u32[]{:S(2)}, u32[]{:S(2)}) collective-permute-start(f32[2,32,256]{2,1,0:T(8,128)S(1)} %pad_maximum_fusion.24), channel_id=1, source_target_pairs={{0,8},{4,12},{8,0},{12,4},{16,24},{20,28},{24,16},{28,20},{1,9},{5... | collective-permute-start | bytes 196616 | tf_op jit(solution)/shard_map/ppermute | solution.py:183
  15.3 1.4 %collective-permute-start.5 = (f32[144,256]{1,0:T(8,128)S(1)}, f32[144,256]{1,0:T(8,128)S(1)}, u32[]{:S(2)}, u32[]{:S(2)}) collective-permute-start(f32[144,256]{1,0:T(8,128)S(1)} %pad_maximum_fusion.14), channel_id=1, source_target_pairs={{0,4},{4,0},{8,12},{12,8},{16,20},{20,16},{24,28},{28,24},{1,5},{5... | collective-permute-start | bytes 442376 | tf_op jit(solution)/shard_map/ppermute | solution.py:183
  28.5 1.4 %collective-permute-start.6 = (f32[144,256]{1,0:T(8,128)S(1)}, f32[144,256]{1,0:T(8,128)S(1)}, u32[]{:S(2)}, u32[]{:S(2)}) collective-permute-start(f32[144,256]{1,0:T(8,128)S(1)} %get-tuple-element.17), channel_id=1, source_target_pairs={{0,4},{4,0},{8,12},{12,8},{16,20},{20,16},{24,28},{28,24},{1,5},{5... | collective-permute-start | bytes 442376 | tf_op jit(solution)/shard_map/ppermute | solution.py:183
  30.0 4.6 %collective-permute-start.7 = (f32[80,256]{1,0:T(8,128)S(1)}, f32[80,256]{1,0:T(8,128)S(1)}, u32[]{:S(2)}, u32[]{:S(2)}) collective-permute-start(f32[80,256]{1,0:T(8,128)S(1)} %get-tuple-element.64), channel_id=1, source_target_pairs={{0,1},{1,0},{2,3},{3,2},{4,5},{5,4},{6,7},{7,6},{8,9},{9,8},{10,11... | collective-permute-start | bytes 245768 | tf_op jit(solution)/shard_map/ppermute | solution.py:183
  31.6 5.3 %collective-permute-start.8 = (f32[80,256]{1,0:T(8,128)S(1)}, f32[80,256]{1,0:T(8,128)S(1)}, u32[]{:S(2)}, u32[]{:S(2)}) collective-permute-start(f32[80,256]{1,0:T(8,128)S(1)} %get-tuple-element.65), channel_id=1, source_target_pairs={{0,2},{1,3},{2,0},{3,1},{4,6},{5,7},{6,4},{7,5},{8,10},{9,11},{10,... | collective-permute-start | bytes 245768 | tf_op jit(solution)/shard_map/ppermute | solution.py:183
  33.1 5.3 %collective-permute-start.9 = (f32[80,256]{1,0:T(8,128)S(1)}, f32[80,256]{1,0:T(8,128)S(1)}, u32[]{:S(2)}, u32[]{:S(2)}) collective-permute-start(f32[80,256]{1,0:T(8,128)S(1)} %get-tuple-element.63), channel_id=1, source_target_pairs={{0,3},{1,2},{2,1},{3,0},{4,7},{5,6},{6,5},{7,4},{8,11},{9,10},{10,... | collective-permute-start | bytes 245768 | tf_op jit(solution)/shard_map/ppermute | solution.py:183
  38.5 5.2 %collective-permute-start.10 = (f32[64,256]{1,0:T(8,128)S(1)}, f32[64,256]{1,0:T(8,128)S(1)}, u32[]{:S(2)}, u32[]{:S(2)}) collective-permute-start(f32[64,256]{1,0:T(8,128)S(1)} %fusion.9), channel_id=1, source_target_pairs={{0,1},{1,0},{2,3},{3,2},{4,5},{5,4},{6,7},{7,6},{8,9},{9,8},{10,11... | collective-permute-start | bytes 196616 | tf_op jit(solution)/shard_map/ppermute | solution.py:183
  39.1 4.6 %collective-permute-start.11 = (f32[64,256]{1,0:T(8,128)S(1)}, f32[64,256]{1,0:T(8,128)S(1)}, u32[]{:S(2)}, u32[]{:S(2)}) collective-permute-start(f32[64,256]{1,0:T(8,128)S(1)} %fusion.9), channel_id=1, source_target_pairs={{0,2},{1,3},{2,0},{3,1},{4,6},{5,7},{6,4},{7,5},{8,10},{9,11},{10,... | collective-permute-start | bytes 196616 | tf_op jit(solution)/shard_map/ppermute | solution.py:183
  40.0 5.2 %collective-permute-start.12 = (f32[64,256]{1,0:T(8,128)S(1)}, f32[64,256]{1,0:T(8,128)S(1)}, u32[]{:S(2)}, u32[]{:S(2)}) collective-permute-start(f32[64,256]{1,0:T(8,128)S(1)} %fusion.9), channel_id=1, source_target_pairs={{0,3},{1,2},{2,1},{3,0},{4,7},{5,6},{6,5},{7,4},{8,11},{9,10},{10,... | collective-permute-start | bytes 196616 | tf_op jit(solution)/shard_map/ppermute | solution.py:183
  42.1 5.2 %collective-permute-start.13 = (f32[144,256]{1,0:T(8,128)S(1)}, f32[144,256]{1,0:T(8,128)S(1)}, u32[]{:S(2)}, u32[]{:S(2)}) collective-permute-start(f32[144,256]{1,0:T(8,128)S(1)} %pad_maximum_fusion.15), channel_id=1, source_target_pairs={{0,8},{4,12},{8,0},{12,4},{16,24},{20,28},{24,16},{28,20},{1,9},{5... | collective-permute-start | bytes 442376 | tf_op jit(solution)/shard_map/ppermute | solution.py:183
  47.3 7.1 %collective-permute-start.14 = (f32[144,256]{1,0:T(8,128)S(1)}, f32[144,256]{1,0:T(8,128)S(1)}, u32[]{:S(2)}, u32[]{:S(2)}) collective-permute-start(f32[144,256]{1,0:T(8,128)S(1)} %fusion.17), channel_id=1, source_target_pairs={{0,24},{4,28},{8,16},{12,20},{16,8},{20,12},{24,0},{28,4},{1,25},{... | collective-permute-start | bytes 442376 | tf_op jit(solution)/shard_map/ppermute | solution.py:183
  54.5 1.4 %collective-permute-start.15 = (f32[144,256]{1,0:T(8,128)S(1)}, f32[144,256]{1,0:T(8,128)S(1)}, u32[]{:S(2)}, u32[]{:S(2)}) collective-permute-start(f32[144,256]{1,0:T(8,128)S(1)} %pad_maximum_fusion.16), channel_id=1, source_target_pairs={{0,4},{4,0},{8,12},{12,8},{16,20},{20,16},{24,28},{28,24},{1,5},{5... | collective-permute-start | bytes 442376 | tf_op jit(solution)/shard_map/ppermute | solution.py:183
  67.8 1.4 %collective-permute-start.16 = (f32[144,256]{1,0:T(8,128)S(1)}, f32[144,256]{1,0:T(8,128)S(1)}, u32[]{:S(2)}, u32[]{:S(2)}) collective-permute-start(f32[144,256]{1,0:T(8,128)S(1)} %get-tuple-element.20), channel_id=1, source_target_pairs={{0,4},{4,0},{8,12},{12,8},{16,20},{20,16},{24,28},{28,24},{1,5},{5... | collective-permute-start | bytes 442376 | tf_op jit(solution)/shard_map/ppermute | solution.py:183
  69.3 4.9 %collective-permute-start.17 = (f32[80,256]{1,0:T(8,128)S(1)}, f32[80,256]{1,0:T(8,128)S(1)}, u32[]{:S(2)}, u32[]{:S(2)}) collective-permute-start(f32[80,256]{1,0:T(8,128)S(1)} %get-tuple-element.61), channel_id=1, source_target_pairs={{0,1},{1,0},{2,3},{3,2},{4,5},{5,4},{6,7},{7,6},{8,9},{9,8},{10,11... | collective-permute-start | bytes 245768 | tf_op jit(solution)/shard_map/ppermute | solution.py:183
  69.9 5.3 %collective-permute-start.18 = (f32[80,256]{1,0:T(8,128)S(1)}, f32[80,256]{1,0:T(8,128)S(1)}, u32[]{:S(2)}, u32[]{:S(2)}) collective-permute-start(f32[80,256]{1,0:T(8,128)S(1)} %get-tuple-element.62), channel_id=1, source_target_pairs={{0,2},{1,3},{2,0},{3,1},{4,6},{5,7},{6,4},{7,5},{8,10},{9,11},{10,... | collective-permute-start | bytes 245768 | tf_op jit(solution)/shard_map/ppermute | solution.py:183
  70.8 5.3 %collective-permute-start.19 = (f32[80,256]{1,0:T(8,128)S(1)}, f32[80,256]{1,0:T(8,128)S(1)}, u32[]{:S(2)}, u32[]{:S(2)}) collective-permute-start(f32[80,256]{1,0:T(8,128)S(1)} %get-tuple-element.60), channel_id=1, source_target_pairs={{0,3},{1,2},{2,1},{3,0},{4,7},{5,6},{6,5},{7,4},{8,11},{9,10},{10,... | collective-permute-start | bytes 245768 | tf_op jit(solution)/shard_map/ppermute | solution.py:183
  76.2 5.2 %collective-permute-start.20 = (f32[48,256]{1,0:T(8,128)S(1)}, f32[48,256]{1,0:T(8,128)S(1)}, u32[]{:S(2)}, u32[]{:S(2)}) collective-permute-start(f32[48,256]{1,0:T(8,128)S(1)} %get-tuple-element.58), channel_id=1, source_target_pairs={{0,8},{4,12},{8,0},{12,4},{16,24},{20,28},{24,16},{28,20},{1,9},{5... | collective-permute-start | bytes 147464 | tf_op jit(solution)/shard_map/ppermute | solution.py:183
  77.8 6.6 %collective-permute-start.21 = (f32[48,256]{1,0:T(8,128)S(1)}, f32[48,256]{1,0:T(8,128)S(1)}, u32[]{:S(2)}, u32[]{:S(2)}) collective-permute-start(f32[48,256]{1,0:T(8,128)S(1)} %get-tuple-element.59), channel_id=1, source_target_pairs={{0,16},{4,20},{8,24},{12,28},{16,0},{20,4},{24,8},{28,12},{1,17},{... | collective-permute-start | bytes 147464 | tf_op jit(solution)/shard_map/ppermute | solution.py:183
  80.4 5.9 %collective-permute-start.22 = (f32[48,256]{1,0:T(8,128)S(1)}, f32[48,256]{1,0:T(8,128)S(1)}, u32[]{:S(2)}, u32[]{:S(2)}) collective-permute-start(f32[48,256]{1,0:T(8,128)S(1)} %get-tuple-element.57), channel_id=1, source_target_pairs={{0,24},{4,28},{8,16},{12,20},{16,8},{20,12},{24,0},{28,4},{1,25},{... | collective-permute-start | bytes 147464 | tf_op jit(solution)/shard_map/ppermute | solution.py:183
  86.3 1.2 %collective-permute-start.23 = (f32[16,256]{1,0:T(8,128)S(1)}, f32[16,256]{1,0:T(8,128)S(1)}, u32[]{:S(2)}, u32[]{:S(2)}) collective-permute-start(f32[16,256]{1,0:T(8,128)S(1)} %fusion.14), channel_id=1, source_target_pairs={{0,4},{4,0},{8,12},{12,8},{16,20},{20,16},{24,28},{28,24},{1,5},{5... | collective-permute-start | bytes 49160 | tf_op jit(solution)/shard_map/ppermute | solution.py:183
  (2 other events, 31.5 us)
